TPU v7x, 768 devices: a whole 4x8x12 slice. The times are simulated.
768 devices in a mesh: mem: 24 (over z, core), reg: 32 (over x, y).
Axes of the slice: x: 4, y: 8, z: 12, core: 2. Of those that a mesh axis runs over, the one named last changes fastest.
Arguments:
- background: bfloat16 [240, 32, 24576], P('mem', 'reg'), may hold values from -6 to 6
- obs_index: int32 [32, 24, 512], P('reg'), may hold values from 0 to 1023
- yobs: bfloat16 [32, 24, 512], P('reg', 'mem'), may hold values from -6 to 6
- loc_list: int32 [32, 24, 2048], P('reg', 'mem'), may hold values from 0 to 4607, as said below
- loc_count: int32 [32, 24], P('reg', 'mem'), may hold values from 256 to 2048, as said below
- loc_weight: float32 [32, 24, 2048], P('reg', 'mem'), may hold values from 0.03 to 0.6
Outputs:
- analysis: bfloat16 [240, 32, 24576], P('mem', 'reg')
Inputs may be any that keep to these rules, and one draw needn't show every extreme that they name: `loc_list`: for each region the first loc_count entries name distinct candidates; later entries are candidate numbers that carry no weight. `loc_count`: some region has exactly 2048 entries and some exactly 256.
All inputs are finite; a program needn't handle non-finite values.
Results may differ from a plain program's by a relative error of at most 0.006.
Values may be sent and summed in bfloat16 or wider, within the bound.
No kernel may reach another device: no remote copies, remote signals or barrier semaphores. Data moves between devices by JAX's collectives and lax.ppermute only.
A program may use at most 64 MiB of HBM per device.

v0:
```python
import math

import jax
import jax.numpy as jnp
from jax import lax
from jax.sharding import PartitionSpec as P

NS_STEPS = 5


inflation = 1.1


def with_halo(shard, sides, width):
    for axis, dim in sides:
        size, length = (lax.axis_size(axis), shard.shape[dim])
        up = [(i, (i + 1) % size) for i in range(size)]
        down = [(j, i) for i, j in up]
        last = lax.slice_in_dim(shard, length - width, length, axis=dim)
        initial = lax.slice_in_dim(shard, 0, width, axis=dim)
        before = lax.ppermute(last, axis, up)
        after = lax.ppermute(initial, axis, down)
        shard = jnp.concatenate([before, shard, after], axis=dim)
    return shard


def observe(states, indices):
    cell_count = states.shape[2]
    by_region = jnp.transpose(states, (1, 0, 2))

    def one_region(pair):
        region_cells, region_indices = pair
        cell_ids = lax.broadcasted_iota(jnp.int32, (cell_count, region_indices.shape[0]), 0)
        picker = (cell_ids == region_indices[None, :]).astype(jnp.bfloat16)
        return jnp.dot(region_cells, picker, preferred_element_type=jnp.float32).astype(
            jnp.bfloat16
        )

    picked = lax.map(one_region, (by_region, indices))
    return jnp.transpose(picked, (1, 0, 2))


def newton_root(gram_matrix):
    size = gram_matrix.shape[0]
    identity = jnp.eye(size, dtype=jnp.float32)
    norm_value = jnp.sqrt(jnp.sum(gram_matrix * gram_matrix))
    current = gram_matrix / norm_value
    inverse_root = identity
    for iteration in range(NS_STEPS):
        correction = 1.5 * identity - 0.5 * jnp.dot(
            inverse_root, current, precision=lax.Precision.HIGHEST
        )
        current = jnp.dot(current, correction, precision=lax.Precision.HIGHEST)
        inverse_root = jnp.dot(correction, inverse_root, precision=lax.Precision.HIGHEST)
    return (inverse_root, norm_value)


def row_products(left_rows, right_rows):
    return lax.dot_general(
        left_rows, right_rows, (((0,), (0,)), ((), ())), preferred_element_type=jnp.float32
    )


def member_mean(rows):
    members = rows.shape[0]
    ones_row = jnp.ones((members,), jnp.bfloat16)
    return jnp.dot(ones_row, rows, preferred_element_type=jnp.float32) / members


def list_products(weighted, local_rows, local_innov):
    gram_matrix = row_products(weighted, local_rows)
    drive_vector = row_products(weighted, local_innov)
    return (gram_matrix, drive_vector)


def analyze(own_state, candidates, obs_order, obs_count, obs_taper):
    members = own_state.shape[0]
    state_mean = member_mean(own_state)
    state_pert = (own_state - state_mean).astype(jnp.bfloat16)
    ensemble = candidates[:members]
    obs_mean = member_mean(ensemble)
    obs_pert = (ensemble - obs_mean).astype(jnp.bfloat16)
    innovation = (candidates[members] - obs_mean).astype(jnp.bfloat16)
    pert_rows = jnp.transpose(obs_pert)
    local_rows = jnp.take(pert_rows, obs_order, axis=0)
    local_innov = jnp.take(innovation, obs_order)
    positions = jnp.arange(obs_order.shape[0], dtype=jnp.int32)
    live_weight = jnp.where(positions < obs_count, obs_taper, jnp.float32(0.0))
    weighted = (local_rows * live_weight[:, None]).astype(jnp.bfloat16)
    gram_matrix, drive_vector = list_products(weighted, local_rows, local_innov)
    gram_matrix = gram_matrix + (members - 1) / inflation * jnp.eye(members, dtype=jnp.float32)
    inverse_root, norm_value = newton_root(gram_matrix)
    mean_shift = jnp.dot(
        inverse_root,
        jnp.dot(inverse_root, drive_vector, precision=lax.Precision.HIGHEST),
        precision=lax.Precision.HIGHEST,
    )
    weights = (
        math.sqrt(members - 1) / jnp.sqrt(norm_value) * inverse_root
        + (mean_shift / norm_value)[:, None]
    )
    weights = weights.astype(jnp.bfloat16)
    update = jnp.dot(weights.T, state_pert, preferred_element_type=jnp.float32)
    return (state_mean + update).astype(jnp.bfloat16)


def local(background, obs_index, yobs, loc_list, loc_count, loc_weight):
    member_share = background.shape[0]
    row_count = obs_index.shape[1]
    cell_count = background.shape[2] // row_count
    region_count = yobs.shape[1]
    obs_width = yobs.shape[2]
    own_cells = background.reshape(member_share, row_count, cell_count)
    observed = observe(own_cells, obs_index[0]).reshape(member_share, 1, row_count * obs_width)
    state, observed = (
        lax.all_to_all(background, "mem", split_axis=2, concat_axis=0, tiled=True),
        lax.all_to_all(observed, "mem", split_axis=2, concat_axis=0, tiled=True),
    )
    ensemble_size = state.shape[0]
    observed = observed.reshape(ensemble_size, 1, region_count, obs_width)
    stacked = jnp.concatenate([observed, yobs.reshape(1, 1, region_count, obs_width)], axis=0)
    extended = with_halo(stacked, (("mem", 2), ("reg", 1)), 1)
    candidates = extended.reshape(ensemble_size + 1, 9 * obs_width)
    results = [
        analyze(state[:, 0, :], candidates, loc_list[0, 0], loc_count[0, 0], loc_weight[0, 0])
    ]
    analysis = jnp.stack(results, axis=1)
    return lax.all_to_all(analysis, "mem", split_axis=0, concat_axis=2, tiled=True)


def solution(mesh):
    return jax.shard_map(
        local,
        mesh=mesh,
        in_specs=(
            P("mem", "reg", None),
            P("reg", None, None),
            P("reg", "mem", None),
            P("reg", "mem", None),
            P("reg", "mem"),
            P("reg", "mem", None),
        ),
        out_specs=P("mem", "reg", None),
        check_vma=False,
    )
```

profile of v0, /device:TPU:1, one launch (start us, length us, event | category | flops | bytes accessed | tf_op | source)
XLA Modules:
  0.0 475.1 jit_solution(6857121259136728335)
XLA Ops:
  0.0 1.6 copy.47
  1.9 28.1 %while.10 = (s32[]{:T(128)}, bf16[24,10,512]{2,1,0:T(8,128)(2,1)S(1)}, bf16[24,10,1024]{2,1,0:T(8,128)(2,1)S(1)}, s32[24,512]{1,0:T(8,128)}, s32[]{:T(128)}) while((s32[]{:T(128)}, bf16[24,10,512]{2,1,0:T(8,128)(2,1)S(1)}, bf16[24,10,1024]{2,1,0:T(8,128)(2,1)S(1)}, s32[24,512]{1,0:T(8,128)}, s32[]{:T(128)}) %tuple.28), condition=%wide.region_1.2_spmd, body=%wide.region_0.1_spmd.sunk | while | flops 11015170 | bytes 56393 | solution.py:39
  1.9 0.7 constant_dynamic-slice_fusion.2
  3.1 0.7 constant_dynamic-slice_fusion.2
  4.3 0.7 constant_dynamic-slice_fusion.2
  5.4 0.7 constant_dynamic-slice_fusion.2
  6.6 0.7 constant_dynamic-slice_fusion.2
  7.8 0.7 constant_dynamic-slice_fusion.2
  8.9 0.7 constant_dynamic-slice_fusion.2
  10.1 0.7 constant_dynamic-slice_fusion.2
  11.3 0.7 constant_dynamic-slice_fusion.2
  14.8 0.7 constant_dynamic-slice_fusion.2
  18.3 0.7 constant_dynamic-slice_fusion.2
  19.5 0.7 constant_dynamic-slice_fusion.2
  21.8 0.7 constant_dynamic-slice_fusion.2
  23.0 0.7 constant_dynamic-slice_fusion.2
  25.3 0.7 constant_dynamic-slice_fusion.2
  26.5 0.7 constant_dynamic-slice_fusion.2
  28.8 0.7 constant_dynamic-slice_fusion.2
  30.3 9.9 %copy.38 = bf16[10,1,12288]{0,1,2:T(2,128)(2,1)} copy(bf16[10,1,12288]{2,0,1:T(8,128)(2,1)S(1)} %reshape.67) | data formatting | bytes 491520 | tf_op jit(solution)/shard_map/reshape | solution.py:114
  40.7 66.9 %reduce.6 = bf16[12288,10]{1,0:T(8,128)(2,1)S(1)} reduce(bf16[12288,1,10]{2,1,0:T(2,128)(2,1)} %bitcast.113, bf16[]{:T(256)} %broadcast.86), dimensions={1}, to_apply=%bitcast.71.reduce_sub_computation | reduce | bytes 491522
  107.7 6.1 %reshape.102 = bf16[24,2,2560]{2,1,0:T(2,128)(2,1)} reshape(bf16[12288,10]{1,0:T(8,128)(2,1)S(1)} %reduce.6) | data formatting | bytes 491520
  113.8 16.7 %all-to-all-start.1 = ((bf16[24,2,2560]{2,1,0:T(2,128)(2,1)}), bf16[24,2,2560]{2,1,0:T(2,128)(2,1)S(1)}, u32[]{:S(2)}, u32[]{:S(2)}) async-start(bf16[24,2,2560]{2,1,0:T(2,128)(2,1)} %reshape.102), calls=%async_computation.1 | async-start | bytes 491520 | tf_op jit(solution)/shard_map/all_to_all | solution.py:117
  130.5 23.0 %copy.33 = bf16[10,1,24576]{0,1,2:T(2,128)(2,1)} copy(bf16[10,1,24576]{2,0,1:T(8,128)(2,1)} %param.8) | data formatting | bytes 983040 | tf_op args[0]
  153.5 134.9 %reduce.5 = bf16[24576,10]{1,0:T(8,128)(2,1)} reduce(bf16[24576,1,10]{2,1,0:T(2,128)(2,1)} %bitcast.112, bf16[]{:T(256)} %broadcast.86), dimensions={1}, to_apply=%bitcast.69.reduce_sub_computation | reduce | bytes 983042
  288.4 11.3 %reshape.100 = bf16[24,2,5120]{2,1,0:T(2,128)(2,1)} reshape(bf16[24576,10]{1,0:T(8,128)(2,1)} %reduce.5) | data formatting | bytes 983040
  299.7 9.7 %all-to-all-start = ((bf16[24,2,5120]{2,1,0:T(2,128)(2,1)}), bf16[24,2,5120]{2,1,0:T(2,128)(2,1)S(1)}, u32[]{:S(2)}, u32[]{:S(2)}) async-start(bf16[24,2,5120]{2,1,0:T(2,128)(2,1)} %reshape.100), calls=%async_computation | async-start | bytes 983040 | tf_op jit(solution)/shard_map/all_to_all | solution.py:116
  309.4 12.2 %reshape.103 = bf16[12288,1,10]{2,1,0:T(2,128)(2,1)} reshape(bf16[24,2,2560]{2,1,0:T(2,128)(2,1)S(1)} %all-to-all-done.1) | data formatting | bytes 491520
  321.5 11.8 %copy.39 = bf16[10,1,12288]{2,0,1:T(8,128)(2,1)S(1)} copy(bf16[10,1,12288]{0,1,2:T(2,128)(2,1)} %bitcast.114) | data formatting | bytes 491520 | tf_op jit(solution)/shard_map/all_to_all | solution.py:117
  334.3 1.6 collective-permute-start
  337.1 2.7 collective-permute-done.1
  339.8 1.0 pad_maximum_fusion.1
  340.8 7.3 %collective-permute-start.3 = (bf16[241,1,3,512]{3,0,2,1:T(8,128)(2,1)}, bf16[241,1,3,512]{3,0,2,1:T(8,128)(2,1)S(1)}, u32[]{:S(2)}, u32[]{:S(2)}) collective-permute-start(bf16[241,1,3,512]{3,0,2,1:T(8,128)(2,1)} %pad_maximum_fusion.1), channel_id=1, source_target_pairs={{1,0},{2,1},{3,2},{4,3},{5,4},{6,5},{7,6},{8,7},{9,8},{10,9},{11,1... | collective-permute-start | bytes 2221064 | tf_op jit(solution)/shard_map/ppermute | solution.py:22
  348.1 1.9 collective-permute-start.2
  350.6 17.4 %reshape.101 = bf16[24576,1,10]{2,1,0:T(2,128)(2,1)} reshape(bf16[24,2,5120]{2,1,0:T(2,128)(2,1)S(1)} %all-to-all-done) | data formatting | bytes 983040
  368.0 23.4 %copy.34 = bf16[10,1,24576]{2,0,1:T(8,128)(2,1)S(1)} copy(bf16[10,1,24576]{0,1,2:T(2,128)(2,1)} %bitcast.111) | data formatting | bytes 983040 | tf_op jit(solution)/shard_map/all_to_all | solution.py:116
  393.1 0.7 fusion.27
  394.7 1.6 slice.17
  396.3 2.8 copy.42
  399.1 1.4 copy-done
  401.3 3.2 fusion.8
  404.6 9.0 %gather_fusion = bf16[2048,240]{1,0:T(8,128)(2,1)} fusion(bf16[4608,240]{1,0:T(8,128)(2,1)S(1)} %fusion.8, s32[2048]{0:T(1024)S(1)} %copy-done.3), kind=kCustom, calls=%fused_computation | custom fusion | bytes 1974272 | tf_op jit(solution)/shard_map/jit(_take)/gather | solution.py:85
  413.6 13.3 %gather_fusion.1 = bf16[2048]{0:T(1024)(128)(2,1)S(1)} fusion(bf16[4608]{0:T(1024)(128)(2,1)S(1)} %get-tuple-element.54, s32[2048]{0:T(1024)S(1)} %copy-done.3), kind=kCustom, calls=%fused_computation.1 | custom fusion | bytes 16384 | tf_op jit(solution)/shard_map/jit(_take)/gather | solution.py:86
  426.9 1.9 multiply_reduce_fusion
  436.5 1.0 reduce.7
  437.8 32.4 %all_to_all.48 = bf16[24,2,5120]{2,1,0:T(2,128)(2,1)S(1)} all-to-all(bf16[24,2,5120]{2,1,0:T(2,128)(2,1)S(1)} %reshape.104), channel_id=1, replica_groups=mesh['mem'=24,'reg'=32] {'mem'}, dimensions={0} | all-to-all | bytes 983040 | tf_op jit(solution)/shard_map/all_to_all | solution.py:128
  470.6 2.9 reduce.2
  473.9 1.2 all_to_all.44
  (107 shorter events, 30.2 us)
Async XLA Ops:
  113.8 185.9 %all-to-all-start.1 = ((bf16[24,2,2560]{2,1,0:T(2,128)(2,1)}), bf16[24,2,2560]{2,1,0:T(2,128)(2,1)S(1)}, u32[]{:S(2)}, u32[]{:S(2)}) async-start(bf16[24,2,2560]{2,1,0:T(2,128)(2,1)} %reshape.102), calls=%async_computation.1 | async-start | bytes 491520 | tf_op jit(solution)/shard_map/all_to_all | solution.py:117
  299.7 50.9 %all-to-all-start = ((bf16[24,2,5120]{2,1,0:T(2,128)(2,1)}), bf16[24,2,5120]{2,1,0:T(2,128)(2,1)S(1)}, u32[]{:S(2)}, u32[]{:S(2)}) async-start(bf16[24,2,5120]{2,1,0:T(2,128)(2,1)} %reshape.100), calls=%async_computation | async-start | bytes 983040 | tf_op jit(solution)/shard_map/all_to_all | solution.py:116
  333.4 0.7 copy-start.6
  333.4 2.5 copy-start.4
  333.4 16.6 %copy-start.8 = (f32[1,1,2048]{2,1,0:T(1,128)S(1)}, f32[1,1,2048]{2,1,0:T(1,128)}, u32[]{:S(2)}) copy-start(f32[1,1,2048]{2,1,0:T(1,128)} %param.13) | copy-start | bytes 24580
  334.1 5.7 %collective-permute-start.1 = (bf16[241,1,1,512]{3,0,2,1:T(8,128)(2,1)S(1)}, bf16[241,1,1,512]{3,0,2,1:T(8,128)(2,1)S(1)}, u32[]{:S(2)}, u32[]{:S(2)}) collective-permute-start(bf16[241,1,1,512]{3,0,2,1:T(8,128)(2,1)S(1)} %pad_maximum_fusion.2), channel_id=1, source_target_pairs={{32,0},{64,32},{96,64},{128,96},{160,128},{192,160},{224,192},{256... | collective-permute-start | bytes 740360 | tf_op jit(solution)/shard_map/ppermute | solution.py:22
  334.3 5.5 %collective-permute-start = (bf16[241,1,1,512]{3,0,2,1:T(8,128)(2,1)S(1)}, bf16[241,1,1,512]{3,0,2,1:T(8,128)(2,1)S(1)}, u32[]{:S(2)}, u32[]{:S(2)}) collective-permute-start(bf16[241,1,1,512]{3,0,2,1:T(8,128)(2,1)S(1)} %pad_maximum_fusion.2), channel_id=1, source_target_pairs={{0,32},{32,64},{64,96},{96,128},{128,160},{160,192},{192,224},{224... | collective-permute-start | bytes 740360 | tf_op jit(solution)/shard_map/ppermute | solution.py:21
  340.8 52.3 %collective-permute-start.3 = (bf16[241,1,3,512]{3,0,2,1:T(8,128)(2,1)}, bf16[241,1,3,512]{3,0,2,1:T(8,128)(2,1)S(1)}, u32[]{:S(2)}, u32[]{:S(2)}) collective-permute-start(bf16[241,1,3,512]{3,0,2,1:T(8,128)(2,1)} %pad_maximum_fusion.1), channel_id=1, source_target_pairs={{1,0},{2,1},{3,2},{4,3},{5,4},{6,5},{7,6},{8,7},{9,8},{10,9},{11,1... | collective-permute-start | bytes 2221064 | tf_op jit(solution)/shard_map/ppermute | solution.py:22
  348.1 45.0 %collective-permute-start.2 = (bf16[241,1,3,512]{3,0,2,1:T(8,128)(2,1)}, bf16[241,1,3,512]{3,0,2,1:T(8,128)(2,1)S(1)}, u32[]{:S(2)}, u32[]{:S(2)}) collective-permute-start(bf16[241,1,3,512]{3,0,2,1:T(8,128)(2,1)} %pad_maximum_fusion.1), channel_id=1, source_target_pairs={{0,1},{1,2},{2,3},{3,4},{4,5},{5,6},{6,7},{7,8},{8,9},{9,10},{10,1... | collective-permute-start | bytes 2221064 | tf_op jit(solution)/shard_map/ppermute | solution.py:21
  392.3 2.1 copy-start.7
  396.3 5.0 %copy-start.2 = (f32[4608]{0:T(1024)S(1)}, f32[4608]{0:T(1024)}, u32[]{:S(2)}) copy-start(f32[4608]{0:T(1024)} %reshape.70) | copy-start | bytes 55300
  399.1 1.4 copy-start
  401.3 3.3 copy-start.3
  413.6 13.3 %copy-start.5 = (s32[1,1,2048]{2,1,0:T(1,128)S(1)}, s32[1,1,2048]{2,1,0:T(1,128)}, u32[]{:S(2)}) copy-start(s32[1,1,2048]{2,1,0:T(1,128)} %param.11) | copy-start | bytes 24580
  413.6 13.3 %copy-start.1 = (bf16[2048,240]{1,0:T(8,128)(2,1)S(1)}, bf16[2048,240]{1,0:T(8,128)(2,1)}, u32[]{:S(2)}) copy-start(bf16[2048,240]{1,0:T(8,128)(2,1)} %gather_fusion) | copy-start | bytes 2949124
  413.6 13.3 %copy-start.9 = (f32[2048]{0:T(1024)S(1)}, f32[2048]{0:T(1024)}, u32[]{:S(2)}) copy-start(f32[2048]{0:T(1024)} %fusion.28) | copy-start | bytes 24580
  433.6 2.6 copy-start.10
where the time goes:
time: 481 us; the launch traced here: 475 us
  other arithmetic  213 us (44%)
  local copies, waits for them, and re-layouts  168 us (35%)
  starting transfers between devices  37.3 us (8%)
  blocking collectives  32.4 us (7%)
  matrix products  20.2 us (4%)
    unnamed x2, other arithmetic  202 us
    unnamed x33, local copies, waits for them, and re-layouts  75.1 us
    all_to_all x1, blocking collectives, local(): lax.all_to_all(analysis, 'mem', split_axis=0, concat_axis=2, tiled=True)  32.4 us
    all_to_all x3, local copies, waits for them, and re-layouts, local(): lax.all_to_all(background, 'mem', split_axis=2, concat_axis=0, tiled=True)  23.7 us
    dynamic_slice x24, local copies, waits for them, and re-layouts, observe(): picked = lax.map(one_region, (by_region, indices))  17.4 us
    all_to_all x1, starting transfers between devices, local(): lax.all_to_all(observed, 'mem', split_axis=2, concat_axis=0, tiled=True)  16.7 us
    gather x1, local copies, waits for them, and re-layouts, analyze(): local_innov = jnp.take(innovation, obs_order)  13.3 us
    all_to_all x3, local copies, waits for them, and re-layouts, local(): lax.all_to_all(observed, 'mem', split_axis=2, concat_axis=0, tiled=True)  11.9 us
  transfers between devices with their start and end apart: 6, of which 1 were waited for; matrix products, arithmetic and copies ran while one was open for 50% of the time, Pallas kernels for 0%

commit v1 on v0

v1 whole, which is shorter than its diff:
```python
import functools
import math

import jax
import jax.numpy as jnp
from jax import lax
from jax.experimental import pallas as pl
from jax.experimental.pallas import tpu as pltpu
from jax.sharding import PartitionSpec as P

NS_STEPS = 5
INFLATION = 1.1
LANES = 128
VMEM_LIMIT = 24 * 1024 * 1024

F32 = jnp.float32
BF16 = jnp.bfloat16


def call(body, out_shape, scratch=(), flops=0, nbytes=0):
    return pl.pallas_call(
        body,
        out_shape=out_shape,
        scratch_shapes=list(scratch),
        compiler_params=pltpu.CompilerParams(vmem_limit_bytes=VMEM_LIMIT),
        cost_estimate=pl.CostEstimate(flops=flops, bytes_accessed=nbytes, transcendentals=0),
    )


def dot_nn(a, b):
    return lax.dot_general(a, b, (((1,), (0,)), ((), ())), preferred_element_type=F32)


def dot_nt(a, b):
    return lax.dot_general(a, b, (((1,), (1,)), ((), ())), preferred_element_type=F32)


def dot_tn(a, b):
    return lax.dot_general(a, b, (((0,), (0,)), ((), ())), preferred_element_type=F32)


def halves(x):
    high = x.astype(BF16)
    return high, (x - high.astype(F32)).astype(BF16)


def product(a, b):
    return dot_nn(a[0], b[0]) + (dot_nn(a[0], b[1]) + dot_nn(a[1], b[0]))


def pack_kernel(regions, tiles, x_ref, out_ref, wide):
    members = x_ref.shape[0]
    rows = members * tiles
    for q in range(regions):
        for t in range(tiles):
            start = (q * tiles + t) * LANES
            wide[pl.ds(q * rows + t, members, stride=tiles), :] = x_ref[
                :, start : start + LANES
            ].astype(F32)
        out_ref[q] = wide[q * rows : (q + 1) * rows, :].astype(BF16)


def unpack_kernel(regions, tiles, x_ref, out_ref, wide):
    members = out_ref.shape[0]
    rows = members * tiles
    for q in range(regions):
        wide[q * rows : (q + 1) * rows, :] = x_ref[q].astype(F32)
        for t in range(tiles):
            start = (q * tiles + t) * LANES
            out_ref[:, start : start + LANES] = wide[
                pl.ds(q * rows + t, members, stride=tiles), :
            ].astype(BF16)


def weight_kernel(list_ref, count_ref, weight_ref, out_ref):
    length = list_ref.shape[1]
    rows = out_ref.shape[0]
    order = list_ref[...]
    position = lax.broadcasted_iota(jnp.int32, (1, length), 1)
    live = jnp.where(position < count_ref[...], weight_ref[...], 0.0)
    high = live.astype(BF16)
    rest = live - high.astype(F32)
    middle = rest.astype(BF16)
    low = (rest - middle.astype(F32)).astype(BF16)
    row_of = lax.shift_right_logical(order, 7)
    lane_of = lax.bitwise_and(order, 127)
    at_row = lax.broadcasted_iota(jnp.int32, (rows, length), 0) == row_of
    at_lane = lax.broadcasted_iota(jnp.int32, (LANES, length), 0) == lane_of
    lane_hot = jnp.where(at_lane, 1.0, 0.0).astype(BF16)

    def spread(part):
        return dot_nt(jnp.where(at_row, part.astype(F32), 0.0).astype(BF16), lane_hot)

    out_ref[...] = (spread(high) + spread(middle)) + spread(low)


def observe_kernel(tiles, x_ref, index_ref, yobs_ref, out_ref, wide):
    cells = tiles * LANES
    members = x_ref.shape[0] // tiles
    width = index_ref.shape[1]
    wide[...] = x_ref[...].astype(F32)
    index = index_ref[...]
    observed = jnp.zeros((members, width), F32)
    for t in range(tiles):
        cell = lax.broadcasted_iota(jnp.int32, (LANES, width), 0) + t * LANES
        hot = jnp.where(cell == index, 1.0, 0.0).astype(BF16)
        part = wide[pl.ds(t, members, stride=tiles), :].astype(BF16)
        observed = observed + dot_nn(part, hot)
    mean = jnp.sum(observed, axis=0, keepdims=True) / members
    out_ref[:members, :] = (observed - mean).astype(BF16)
    extra = out_ref.shape[0] - members
    innovation = yobs_ref[...].astype(F32) - mean
    row = lax.broadcasted_iota(jnp.int32, (extra, width), 0)
    out_ref[members:, :] = jnp.where(row == 0, innovation, 0.0).astype(BF16)


def state_kernel(tiles, x_ref, mean_ref, pert_ref, wide):
    members = x_ref.shape[0] // tiles
    wide[...] = x_ref[...].astype(F32)
    for t in range(tiles):
        part = wide[pl.ds(t, members, stride=tiles), :]
        mean = jnp.sum(part, axis=0, keepdims=True) / members
        lanes = slice(t * LANES, (t + 1) * LANES)
        mean_ref[:, lanes] = mean
        pert_ref[:, lanes] = (part - mean).astype(BF16)


def gram_kernel(members, before_ref, own_ref, after_ref, w_ref, wl_ref, wr_ref, own_out, left_out, right_out):
    width = own_ref.shape[1]
    chunks = width // LANES
    blocks = (before_ref, own_ref, after_ref)
    per_col = 3 * chunks
    for weights, first, out in (
        (w_ref, per_col, own_out),
        (wl_ref, 0, left_out),
        (wr_ref, 0, right_out),
    ):
        total = None
        for b in range(3):
            rows = blocks[b][...]
            weight = jnp.concatenate(
                [weights[first + b * chunks + c : first + b * chunks + c + 1, :] for c in range(chunks)],
                axis=1,
            )
            weighted = (rows[:members].astype(F32) * weight).astype(BF16)
            term = dot_nt(weighted, rows)
            total = term if total is None else total + term
        out[...] = total


def update_kernel(members, tiles, g_ref, gl_ref, gr_ref, mean_ref, pert_ref, out_ref, wide):
    total = g_ref[...] + (gl_ref[...] + gr_ref[...])
    row = lax.broadcasted_iota(jnp.int32, (members, members), 0)
    col = lax.broadcasted_iota(jnp.int32, (members, members), 1)
    diagonal = row == col
    gram = total[:, :members] + jnp.where(diagonal, (members - 1) / INFLATION, 0.0)
    tail = total.shape[1] - LANES
    drive = total[:, tail:]
    square = jnp.sum(jnp.sum(gram * gram, axis=1, keepdims=True), axis=0, keepdims=True)
    norm = jnp.sqrt(square)

    def correction_of(zy):
        return jnp.where(diagonal, 1.5, 0.0) - 0.5 * zy

    current = gram / norm
    correction = correction_of(current)
    inverse = correction
    for step in range(1, NS_STEPS + 1):
        m = halves(correction)
        if step > 1:
            inverse = product(m, halves(inverse))
        if step == NS_STEPS:
            break
        current = product(halves(current), m)
        correction = correction_of(product(halves(inverse), halves(current)))
    root = halves(inverse)
    shift = product(root, halves(product(root, halves(drive))))
    shift = shift[:, members - tail : members - tail + 1]
    weights = (math.sqrt(members - 1) / jnp.sqrt(norm) * inverse + shift / norm).astype(BF16)
    update = dot_tn(weights, pert_ref[...])
    for t in range(tiles):
        lanes = slice(t * LANES, (t + 1) * LANES)
        wide[pl.ds(t, members, stride=tiles), :] = mean_ref[:, lanes] + update[:, lanes]
    out_ref[...] = wide[...].astype(BF16)


def local(background, obs_index, yobs, loc_list, loc_count, loc_weight):
    share = background.shape[0]
    regions = obs_index.shape[1]
    cells = background.shape[2] // regions
    width = yobs.shape[2]
    tiles = cells // LANES
    members = share * lax.axis_size("mem")
    rows = share * tiles
    padded = members + 16
    chunks = width // LANES
    cand_rows = 9 * chunks

    def ring(axis):
        size = lax.axis_size(axis)
        up = [(i, (i + 1) % size) for i in range(size)]
        return up, [(j, i) for i, j in up]

    mem_up, mem_down = ring("mem")
    reg_up, reg_down = ring("reg")

    weight = call(
        weight_kernel,
        jax.ShapeDtypeStruct((cand_rows, LANES), F32),
        flops=2 * 3 * cand_rows * 2048 * LANES,
        nbytes=1 << 15,
    )(loc_list[0], loc_count, loc_weight[0])
    weight_right = lax.ppermute(weight[: 3 * chunks], "reg", reg_down)
    weight_left = lax.ppermute(weight[6 * chunks :], "reg", reg_up)

    packed = call(
        functools.partial(pack_kernel, regions, tiles),
        jax.ShapeDtypeStruct((regions, rows, LANES), BF16),
        [pltpu.VMEM((regions * rows, LANES), F32)],
        nbytes=2 * 2 * share * regions * cells,
    )(background.reshape(share, regions * cells))
    state = lax.all_to_all(packed, "mem", split_axis=0, concat_axis=0, tiled=True)
    state = state.reshape(members * tiles, LANES)

    own_row = lax.axis_index("mem")
    index = lax.dynamic_slice_in_dim(obs_index[0], own_row, 1, axis=0)
    wide = [pltpu.VMEM((members * tiles, LANES), F32)]
    observed = call(
        functools.partial(observe_kernel, tiles),
        jax.ShapeDtypeStruct((padded, width), BF16),
        wide,
        flops=2 * members * cells * width,
        nbytes=2 * members * cells,
    )(state, index, yobs[0])
    before = lax.ppermute(observed, "mem", mem_up)
    after = lax.ppermute(observed, "mem", mem_down)
    mean, pert = call(
        functools.partial(state_kernel, tiles),
        (
            jax.ShapeDtypeStruct((1, cells), F32),
            jax.ShapeDtypeStruct((members, cells), BF16),
        ),
        wide,
        flops=4 * members * cells,
        nbytes=4 * members * cells,
    )(state)
    gram_shape = jax.ShapeDtypeStruct((members, padded), F32)
    gram, to_left, to_right = call(
        functools.partial(gram_kernel, members),
        (gram_shape,) * 3,
        flops=18 * members * padded * width,
        nbytes=12 * members * padded,
    )(before, observed, after, weight, weight_left, weight_right)
    gram_a = lax.ppermute(to_left, "reg", reg_down)
    gram_b = lax.ppermute(to_right, "reg", reg_up)
    analysis = call(
        functools.partial(update_kernel, members, tiles),
        jax.ShapeDtypeStruct((members * tiles, LANES), BF16),
        wide,
        flops=2 * members * members * (cells + 40 * members),
        nbytes=4 * members * cells,
    )(gram, gram_a, gram_b, mean, pert)
    returned = lax.all_to_all(
        analysis.reshape(regions, rows, LANES), "mem", split_axis=0, concat_axis=0, tiled=True
    )
    out = call(
        functools.partial(unpack_kernel, regions, tiles),
        jax.ShapeDtypeStruct((share, regions * cells), BF16),
        [pltpu.VMEM((regions * rows, LANES), F32)],
        nbytes=2 * 2 * share * regions * cells,
    )(returned)
    return out.reshape(share, 1, regions * cells)


def solution(mesh):
    return jax.shard_map(
        local,
        mesh=mesh,
        in_specs=(
            P("mem", "reg", None),
            P("reg", None, None),
            P("reg", "mem", None),
            P("reg", "mem", None),
            P("reg", "mem"),
            P("reg", "mem", None),
        ),
        out_specs=P("mem", "reg", None),
        check_vma=False,
    )
```

time: 481 us -> 108 us (0.22); the launches traced: 475 us -> 108 us
  other arithmetic: 213 us -> 0 us
  local copies, waits for them, and re-layouts: 168 us -> 1.17 us
  waiting for transfers between devices: 2.72 us -> 30.1 us
  matrix products: 20.2 us -> 0 us
  Pallas kernels: 0 us -> 8.77 us
    unnamed x2 -> x0, other arithmetic: 202 us -> none
    unnamed x33 -> x10, local copies, waits for them, and re-layouts: 75.1 us -> 1.16 us
    all_to_all x9 -> x0, local copies, waits for them, and re-layouts: 37.2 us -> none  [the longest x3 23.7 us: local(): lax.all_to_all(background, 'mem', split_axis=2, concat_axis=0, tiled=True)]
    gather x2 -> x0, local copies, waits for them, and re-layouts: 22.3 us -> none  [the longest x1 13.3 us: analyze(): local_innov = jnp.take(innovation, obs_order)]
    all_to_all x2 -> x1, waiting for transfers between devices: 0.01 us -> 21.4 us  [local(): lax.all_to_all(packed, 'mem', split_axis=0, concat_axis=0, tiled=True)]
    dot_general x45 -> x0, matrix products: 20.2 us -> none  [the longest x24 10.7 us: one_region(): jnp.dot(region_cells, picker, preferred_element_type=jnp.float32)]
    dynamic_slice x24 -> x1, local copies, waits for them, and re-layouts: 17.4 us -> 0.01 us  [local(): index = lax.dynamic_slice_in_dim(obs_index[0], own_row, 1, axis=0)]
    reshape x3 -> x0, local copies, waits for them, and re-layouts: 10.1 us -> none  [the longest x2 10.1 us: local(): observe(own_cells, obs_index[0])]
  transfers between devices with their start and end apart: 6 -> 7, of which waited for: 1 -> 4; matrix products, arithmetic and copies ran while one was open for 50% -> 0% of each run, Pallas kernels for 0% -> 1%
where the time goes in v1:
time: 108 us
  starting transfers between devices  37.4 us (35%)
  waiting for transfers between devices  30.1 us (28%)
  blocking collectives  29.7 us (28%)
  Pallas kernels  8.77 us (8%)
  local copies, waits for them, and re-layouts  1.17 us (1%)
    all_to_all x1, blocking collectives, local(): lax.all_to_all(analysis.reshape(regions, rows, LANES), 'mem', split_axis=...  29.7 us
    all_to_all x1, waiting for transfers between devices, local(): lax.all_to_all(packed, 'mem', split_axis=0, concat_axis=0, tiled=True)  21.4 us
    all_to_all x1, starting transfers between devices, local(): lax.all_to_all(packed, 'mem', split_axis=0, concat_axis=0, tiled=True)  16.7 us
    ppermute x1, waiting for transfers between devices, local(): gram_b = lax.ppermute(to_right, 'reg', reg_up)  7.14 us
    ppermute x1, starting transfers between devices, local(): gram_a = lax.ppermute(to_left, 'reg', reg_down)  6.94 us
    ppermute x1, starting transfers between devices, local(): weight_right = lax.ppermute(weight[:3 * chunks], 'reg', reg_down)  6.01 us
    pallas_call x1, Pallas kernels, local(): call(functools.partial(update_kernel, members, tiles), jax.ShapeDtypeStru...  3.94 us
    ppermute x1, starting transfers between devices, local(): weight_left = lax.ppermute(weight[6 * chunks:], 'reg', reg_up)  3.2 us
  transfers between devices with their start and end apart: 7, of which 4 were waited for; matrix products, arithmetic and copies ran while one was open for 0% of the time, Pallas kernels for 1%

profile of v1, /device:TPU:1, one launch (start us, length us, event | category | flops | bytes accessed | tf_op | source)
XLA Modules:
  0.0 108.0 jit_solution(6435014215804506676)
XLA Ops:
  0.0 0.0 copy-start
  0.0 0.0 copy-start.1
  0.0 1.1 %copy-done.1 = bf16[10,1,24576]{2,0,1:T(8,128)(2,1)S(1)} copy-done((bf16[10,1,24576]{2,0,1:T(8,128)(2,1)S(1)}, bf16[10,1,24576]{2,0,1:T(8,128)(2,1)}, u32[]{:S(2)}) %copy-start.1) | copy-done | bytes 491544
  1.1 1.0 shard_map.64
  2.2 16.7 %all-to-all-start = ((bf16[24,80,128]{2,1,0:T(8,128)(2,1)}), bf16[24,80,128]{2,1,0:T(8,128)(2,1)S(1)}, u32[]{:S(2)}, u32[]{:S(2)}) async-start(bf16[24,80,128]{2,1,0:T(8,128)(2,1)} %shard_map.64), calls=%async_computation | async-start | bytes 983040 | tf_op jit(solution)/shard_map/all_to_all | solution.py:222
  18.9 0.0 copy-done
  18.9 0.0 copy-start.4
  18.9 21.4 %all-to-all-done = bf16[24,80,128]{2,1,0:T(8,128)(2,1)S(1)} async-done(((bf16[24,80,128]{2,1,0:T(8,128)(2,1)}), bf16[24,80,128]{2,1,0:T(8,128)(2,1)S(1)}, u32[]{:S(2)}, u32[]{:S(2)}) %all-to-all-start) | async-done | bytes 491552 | tf_op jit(solution)/shard_map/all_to_all | solution.py:222
  40.3 0.0 copy-done.4
  40.3 0.0 copy-start.2
  40.3 0.0 copy-start.3
  40.3 0.8 shard_map.65.own_ref
  41.1 0.3 collective-permute-start
  41.3 2.4 %collective-permute-start.1 = (bf16[256,512]{1,0:T(8,128)(2,1)S(1)}, bf16[256,512]{1,0:T(8,128)(2,1)S(1)}, u32[]{:S(2)}, u32[]{:S(2)}) collective-permute-start(bf16[256,512]{1,0:T(8,128)(2,1)S(1)} %shard_map.65.own_ref), channel_id=1, source_target_pairs={{32,0},{64,32},{96,64},{128,96},{160,128},{192,160},{224,192},{256... | collective-permute-start | bytes 786440 | tf_op jit(solution)/shard_map/ppermute | solution.py:236
  44.4 0.0 copy-done.2
  44.4 0.0 copy-done.3
  44.4 0.7 shard_map.66.w_ref
  45.1 3.2 %collective-permute-start.2 = (f32[12,128]{1,0:T(8,128)S(1)}, f32[12,128]{1,0:T(8,128)S(1)}, u32[]{:S(2)}, u32[]{:S(2)}) collective-permute-start(f32[12,128]{1,0:T(8,128)S(1)} %get-tuple-element.16), channel_id=1, source_target_pairs={{0,1},{1,2},{2,3},{3,4},{4,5},{5,6},{6,7},{7,8},{8,9},{9,10},{10,1... | collective-permute-start | bytes 18440 | tf_op jit(solution)/shard_map/ppermute | solution.py:214
  48.3 6.0 %collective-permute-start.3 = (f32[12,128]{1,0:T(8,128)S(1)}, f32[12,128]{1,0:T(8,128)S(1)}, u32[]{:S(2)}, u32[]{:S(2)}) collective-permute-start(f32[12,128]{1,0:T(8,128)S(1)} %get-tuple-element.15), channel_id=1, source_target_pairs={{1,0},{2,1},{3,2},{4,3},{5,4},{6,5},{7,6},{8,7},{9,8},{10,9},{11,1... | collective-permute-start | bytes 18440 | tf_op jit(solution)/shard_map/ppermute | solution.py:213
  54.3 0.0 collective-permute-done.2.wl_ref
  54.3 0.8 collective-permute-done.3.wr_ref
  55.1 0.0 collective-permute-done.before_ref
  55.1 0.0 collective-permute-done.1.after_ref
  55.1 0.8 shard_map.67
  55.9 6.9 %collective-permute-start.4 = (f32[240,256]{1,0:T(8,128)S(1)}, f32[240,256]{1,0:T(8,128)S(1)}, u32[]{:S(2)}, u32[]{:S(2)}) collective-permute-start(f32[240,256]{1,0:T(8,128)S(1)} %get-tuple-element.11), channel_id=1, source_target_pairs={{1,0},{2,1},{3,2},{4,3},{5,4},{6,5},{7,6},{8,7},{9,8},{10,9},{11,1... | collective-permute-start | bytes 737288 | tf_op jit(solution)/shard_map/ppermute | solution.py:254
  62.9 1.9 %collective-permute-start.5 = (f32[240,256]{1,0:T(8,128)S(1)}, f32[240,256]{1,0:T(8,128)S(1)}, u32[]{:S(2)}, u32[]{:S(2)}) collective-permute-start(f32[240,256]{1,0:T(8,128)S(1)} %get-tuple-element.12), channel_id=1, source_target_pairs={{0,1},{1,2},{2,3},{3,4},{4,5},{5,6},{6,7},{7,8},{8,9},{9,10},{10,1... | collective-permute-start | bytes 737288 | tf_op jit(solution)/shard_map/ppermute | solution.py:255
  64.8 0.4 shard_map.68
  65.2 0.8 collective-permute-done.4.gl_ref
  66.0 7.1 %collective-permute-done.5.gr_ref = f32[240,256]{1,0:T(8,128)S(1)} collective-permute-done((f32[240,256]{1,0:T(8,128)S(1)}, f32[240,256]{1,0:T(8,128)S(1)}, u32[]{:S(2)}, u32[]{:S(2)}) %collective-permute-start.5) | collective-permute-done | bytes 245792 | tf_op jit(solution)/shard_map/ppermute | solution.py:255
  73.1 3.9 %shard_map.69 = bf16[1920,128]{1,0:T(8,128)(2,1)S(1)} custom-call(f32[240,256]{1,0:T(8,128)S(1)} %get-tuple-element.10.g_ref, f32[240,256]{1,0:T(8,128)S(1)} %collective-permute-done.4.gl_ref, f32[240,256]{1,0:T(8,128)S(1)} %collective-permute-done.5.gr_ref, f32[1,1024]{1,0:T(1,128)S(1)} %get-tuple-element.13.mean_ref, ...), custom_call_target="tpu_custom_call" | custom-call | flops 1223884800 | bytes 983040 | tf_op jit(solution)/shard_map/pallas_call | solution.py:256
  77.1 29.7 %all_to_all.10.x_ref = bf16[24,80,128]{2,1,0:T(8,128)(2,1)S(1)} all-to-all(bf16[24,80,128]{2,1,0:T(8,128)(2,1)S(1)} %bitcast.12), channel_id=1, replica_groups=mesh['mem'=24,'reg'=32] {'mem'}, dimensions={0} | all-to-all | bytes 983040 | tf_op jit(solution)/shard_map/all_to_all | solution.py:263
  106.8 1.2 %shard_map.70 = bf16[10,24576]{1,0:T(8,128)(2,1)} custom-call(bf16[24,80,128]{2,1,0:T(8,128)(2,1)S(1)} %all_to_all.10.x_ref), custom_call_target="tpu_custom_call" | custom-call | bytes 983040 | tf_op jit(solution)/shard_map/pallas_call | solution.py:266
  (2 shorter events, 0.0 us)
Async XLA Ops:
  0.0 18.9 %copy-start = (s32[1,24,512]{2,1,0:T(8,128)S(1)}, s32[1,24,512]{2,1,0:T(8,128)}, u32[]{:S(2)}) copy-start(s32[1,24,512]{2,1,0:T(8,128)} %param.7) | copy-start | bytes 147460
  0.0 1.1 %copy-start.1 = (bf16[10,1,24576]{2,0,1:T(8,128)(2,1)S(1)}, bf16[10,1,24576]{2,0,1:T(8,128)(2,1)}, u32[]{:S(2)}) copy-start(bf16[10,1,24576]{2,0,1:T(8,128)(2,1)} %param.6) | copy-start | bytes 1474564
  2.2 38.1 %all-to-all-start = ((bf16[24,80,128]{2,1,0:T(8,128)(2,1)}), bf16[24,80,128]{2,1,0:T(8,128)(2,1)S(1)}, u32[]{:S(2)}, u32[]{:S(2)}) async-start(bf16[24,80,128]{2,1,0:T(8,128)(2,1)} %shard_map.64), calls=%async_computation | async-start | bytes 983040 | tf_op jit(solution)/shard_map/all_to_all | solution.py:222
  18.9 21.4 %copy-start.4 = (bf16[1,1,512]{2,1,0:T(2,128)(2,1)S(1)}, bf16[1,1,512]{2,1,0:T(2,128)(2,1)}, u32[]{:S(2)}) copy-start(bf16[1,1,512]{2,1,0:T(2,128)(2,1)} %param.8) | copy-start | bytes 3076
  40.3 4.1 %copy-start.2 = (s32[1,1,2048]{2,1,0:T(1,128)S(1)}, s32[1,1,2048]{2,1,0:T(1,128)}, u32[]{:S(2)}) copy-start(s32[1,1,2048]{2,1,0:T(1,128)} %param.9) | copy-start | bytes 24580
  40.3 4.1 %copy-start.3 = (f32[1,1,2048]{2,1,0:T(1,128)S(1)}, f32[1,1,2048]{2,1,0:T(1,128)}, u32[]{:S(2)}) copy-start(f32[1,1,2048]{2,1,0:T(1,128)} %param.11) | copy-start | bytes 24580
  41.1 14.0 %collective-permute-start = (bf16[256,512]{1,0:T(8,128)(2,1)S(1)}, bf16[256,512]{1,0:T(8,128)(2,1)S(1)}, u32[]{:S(2)}, u32[]{:S(2)}) collective-permute-start(bf16[256,512]{1,0:T(8,128)(2,1)S(1)} %shard_map.65.own_ref), channel_id=1, source_target_pairs={{0,32},{32,64},{64,96},{96,128},{128,160},{160,192},{192,224},{224... | collective-permute-start | bytes 786440 | tf_op jit(solution)/shard_map/ppermute | solution.py:235
  41.3 13.8 %collective-permute-start.1 = (bf16[256,512]{1,0:T(8,128)(2,1)S(1)}, bf16[256,512]{1,0:T(8,128)(2,1)S(1)}, u32[]{:S(2)}, u32[]{:S(2)}) collective-permute-start(bf16[256,512]{1,0:T(8,128)(2,1)S(1)} %shard_map.65.own_ref), channel_id=1, source_target_pairs={{32,0},{64,32},{96,64},{128,96},{160,128},{192,160},{224,192},{256... | collective-permute-start | bytes 786440 | tf_op jit(solution)/shard_map/ppermute | solution.py:236
  45.1 9.2 %collective-permute-start.2 = (f32[12,128]{1,0:T(8,128)S(1)}, f32[12,128]{1,0:T(8,128)S(1)}, u32[]{:S(2)}, u32[]{:S(2)}) collective-permute-start(f32[12,128]{1,0:T(8,128)S(1)} %get-tuple-element.16), channel_id=1, source_target_pairs={{0,1},{1,2},{2,3},{3,4},{4,5},{5,6},{6,7},{7,8},{8,9},{9,10},{10,1... | collective-permute-start | bytes 18440 | tf_op jit(solution)/shard_map/ppermute | solution.py:214
  48.3 6.8 %collective-permute-start.3 = (f32[12,128]{1,0:T(8,128)S(1)}, f32[12,128]{1,0:T(8,128)S(1)}, u32[]{:S(2)}, u32[]{:S(2)}) collective-permute-start(f32[12,128]{1,0:T(8,128)S(1)} %get-tuple-element.15), channel_id=1, source_target_pairs={{1,0},{2,1},{3,2},{4,3},{5,4},{6,5},{7,6},{8,7},{9,8},{10,9},{11,1... | collective-permute-start | bytes 18440 | tf_op jit(solution)/shard_map/ppermute | solution.py:213
  55.9 10.1 %collective-permute-start.4 = (f32[240,256]{1,0:T(8,128)S(1)}, f32[240,256]{1,0:T(8,128)S(1)}, u32[]{:S(2)}, u32[]{:S(2)}) collective-permute-start(f32[240,256]{1,0:T(8,128)S(1)} %get-tuple-element.11), channel_id=1, source_target_pairs={{1,0},{2,1},{3,2},{4,3},{5,4},{6,5},{7,6},{8,7},{9,8},{10,9},{11,1... | collective-permute-start | bytes 737288 | tf_op jit(solution)/shard_map/ppermute | solution.py:254
  62.9 10.3 %collective-permute-start.5 = (f32[240,256]{1,0:T(8,128)S(1)}, f32[240,256]{1,0:T(8,128)S(1)}, u32[]{:S(2)}, u32[]{:S(2)}) collective-permute-start(f32[240,256]{1,0:T(8,128)S(1)} %get-tuple-element.12), channel_id=1, source_target_pairs={{0,1},{1,2},{2,3},{3,4},{4,5},{5,6},{6,7},{7,8},{8,9},{9,10},{10,1... | collective-permute-start | bytes 737288 | tf_op jit(solution)/shard_map/ppermute | solution.py:255

commit v2 on v1

--- a/solution.py
+++ b/solution.py
@@ -12,18 +12,21 @@
 INFLATION = 1.1
 LANES = 128
 VMEM_LIMIT = 24 * 1024 * 1024
+PACK_LIMIT = 60 * 1024 * 1024
+PIECES = 4
 
 F32 = jnp.float32
 BF16 = jnp.bfloat16
 
 
-def call(body, out_shape, scratch=(), flops=0, nbytes=0):
+def call(body, out_shape, scratch=(), flops=0, nbytes=0, limit=VMEM_LIMIT, **specs):
     return pl.pallas_call(
         body,
         out_shape=out_shape,
         scratch_shapes=list(scratch),
-        compiler_params=pltpu.CompilerParams(vmem_limit_bytes=VMEM_LIMIT),
+        compiler_params=pltpu.CompilerParams(vmem_limit_bytes=limit),
         cost_estimate=pl.CostEstimate(flops=flops, bytes_accessed=nbytes, transcendentals=0),
+        **specs,
     )
 
 
@@ -45,31 +48,60 @@
 
 
 def product(a, b):
-    return dot_nn(a[0], b[0]) + (dot_nn(a[0], b[1]) + dot_nn(a[1], b[0]))
-
-
-def pack_kernel(regions, tiles, x_ref, out_ref, wide):
-    members = x_ref.shape[0]
+    return dot_nn(jnp.concatenate([a[1], a[0], a[0]], axis=1), jnp.concatenate([b[0], b[1], b[0]], axis=0))
+
+
+def pack_kernel(regions, tiles, x_hbm, out_hbm, held, wide, made, in_sems, out_sems):
+    members = x_hbm.shape[0]
     rows = members * tiles
-    for q in range(regions):
-        for t in range(tiles):
-            start = (q * tiles + t) * LANES
-            wide[pl.ds(q * rows + t, members, stride=tiles), :] = x_ref[
-                :, start : start + LANES
-            ].astype(F32)
-        out_ref[q] = wide[q * rows : (q + 1) * rows, :].astype(BF16)
-
-
-def unpack_kernel(regions, tiles, x_ref, out_ref, wide):
-    members = out_ref.shape[0]
+    group = regions // PIECES
+    span = group * tiles * LANES
+
+    def taken(piece):
+        lanes = pl.ds(piece * span, span)
+        return pltpu.make_async_copy(x_hbm.at[:, lanes], held.at[:, lanes], in_sems.at[piece])
+
+    def given(piece):
+        part = pl.ds(piece * group, group)
+        return pltpu.make_async_copy(made.at[part], out_hbm.at[part], out_sems.at[piece])
+
+    for piece in range(PIECES):
+        taken(piece).start()
+    for piece in range(PIECES):
+        taken(piece).wait()
+        for q in range(piece * group, (piece + 1) * group):
+            for t in range(tiles):
+                start = (q * tiles + t) * LANES
+                wide[pl.ds(q * rows + t, members, stride=tiles), :] = held[
+                    :, start : start + LANES
+                ].astype(F32)
+            made[q] = wide[q * rows : (q + 1) * rows, :].astype(BF16)
+        given(piece).start()
+    for piece in range(PIECES):
+        given(piece).wait()
+
+
+def unpack_kernel(regions, tiles, x_ref, out_hbm, wide, made, out_sems):
+    members = made.shape[0]
     rows = members * tiles
-    for q in range(regions):
-        wide[q * rows : (q + 1) * rows, :] = x_ref[q].astype(F32)
-        for t in range(tiles):
-            start = (q * tiles + t) * LANES
-            out_ref[:, start : start + LANES] = wide[
-                pl.ds(q * rows + t, members, stride=tiles), :
-            ].astype(BF16)
+    group = regions // PIECES
+    span = group * tiles * LANES
+
+    def given(piece):
+        lanes = pl.ds(piece * span, span)
+        return pltpu.make_async_copy(made.at[:, lanes], out_hbm.at[:, lanes], out_sems.at[piece])
+
+    for piece in range(PIECES):
+        for q in range(piece * group, (piece + 1) * group):
+            wide[q * rows : (q + 1) * rows, :] = x_ref[q].astype(F32)
+            for t in range(tiles):
+                start = (q * tiles + t) * LANES
+                made[:, start : start + LANES] = wide[
+                    pl.ds(q * rows + t, members, stride=tiles), :
+                ].astype(BF16)
+        given(piece).start()
+    for piece in range(PIECES):
+        given(piece).wait()
 
 
 def weight_kernel(list_ref, count_ref, weight_ref, out_ref):
@@ -94,7 +126,7 @@
     out_ref[...] = (spread(high) + spread(middle)) + spread(low)
 
 
-def observe_kernel(tiles, x_ref, index_ref, yobs_ref, out_ref, wide):
+def observe_kernel(tiles, x_ref, index_ref, yobs_ref, wl_ref, wr_ref, out_ref, wide):
     cells = tiles * LANES
     members = x_ref.shape[0] // tiles
     width = index_ref.shape[1]
@@ -114,48 +146,80 @@
     out_ref[members:, :] = jnp.where(row == 0, innovation, 0.0).astype(BF16)
 
 
-def state_kernel(tiles, x_ref, mean_ref, pert_ref, wide):
-    members = x_ref.shape[0] // tiles
+def packed_gram(members, blocks, w_ref, first):
+    chunks = blocks[0].shape[1] // LANES
+    total = None
+    for b in range(3):
+        rows = blocks[b][...]
+        start = first + b * chunks
+        weight = jnp.concatenate([w_ref[start + c : start + c + 1, :] for c in range(chunks)], axis=1)
+        term = dot_nt((rows[:members].astype(F32) * weight).astype(BF16), rows)
+        total = term if total is None else total + term
+    rest = members - LANES
+    row = lax.broadcasted_iota(jnp.int32, (LANES, LANES), 0)
+    col = lax.broadcasted_iota(jnp.int32, (LANES, LANES), 1)
+    spare = jnp.zeros((LANES - rest, LANES), F32)
+    last = jnp.concatenate([total[LANES:, LANES:], spare], axis=0)
+    shifted = pltpu.roll(last, LANES - rest, 1)
+    upper = jnp.where(row >= col, total[:LANES, :LANES], shifted)
+    lower = jnp.where(col == rest + 1, last[:, rest : rest + 1], total[:LANES, LANES:])
+    return jnp.concatenate([upper, lower], axis=0)
+
+
+def unpacked_gram(members, packed):
+    rest = members - LANES
+    row = lax.broadcasted_iota(jnp.int32, (LANES, LANES), 0)
+    col = lax.broadcasted_iota(jnp.int32, (LANES, LANES), 1)
+    upper, middle = packed[:LANES], packed[LANES:]
+    first = jnp.where(row >= col, upper, 0.0)
+    first = first + jnp.where(row > col, upper, 0.0).T
+    last = pltpu.roll(upper, rest, 1)
+    last = jnp.where((row <= col) & (col < rest), last, 0.0)
+    last = last + jnp.where(row < col, last, 0.0).T
+    turned = middle.T
+    gram = jnp.concatenate(
+        [
+            jnp.concatenate([first, jnp.where(col < rest, middle, 0.0)], axis=1),
+            jnp.concatenate([jnp.where(row < rest, turned, 0.0), last], axis=1),
+        ],
+        axis=0,
+    )
+    drive = jnp.concatenate(
+        [
+            turned[rest : rest + 1],
+            jnp.where(col[:1] < rest, turned[rest + 1 : rest + 2], 0.0),
+        ],
+        axis=1,
+    )
+    return gram, drive
+
+
+def neighbour_kernel(members, before_ref, own_ref, after_ref, wl_ref, wr_ref, left_out, right_out):
+    blocks = (before_ref, own_ref, after_ref)
+    left_out[...] = packed_gram(members, blocks, wl_ref, 0)
+    right_out[...] = packed_gram(members, blocks, wr_ref, 0)
+
+
+def own_kernel(members, tiles, before_ref, own_ref, after_ref, w_ref, x_ref, gram_out, mean_ref, pert_ref, wide):
+    gram_out[...] = packed_gram(members, (before_ref, own_ref, after_ref), w_ref, w_ref.shape[0] // 3)
     wide[...] = x_ref[...].astype(F32)
+    extra = pert_ref.shape[0] - members
+    pert_ref[members:, :] = jnp.zeros((extra, pert_ref.shape[1]), BF16)
     for t in range(tiles):
         part = wide[pl.ds(t, members, stride=tiles), :]
         mean = jnp.sum(part, axis=0, keepdims=True) / members
         lanes = slice(t * LANES, (t + 1) * LANES)
         mean_ref[:, lanes] = mean
-        pert_ref[:, lanes] = (part - mean).astype(BF16)
-
-
-def gram_kernel(members, before_ref, own_ref, after_ref, w_ref, wl_ref, wr_ref, own_out, left_out, right_out):
-    width = own_ref.shape[1]
-    chunks = width // LANES
-    blocks = (before_ref, own_ref, after_ref)
-    per_col = 3 * chunks
-    for weights, first, out in (
-        (w_ref, per_col, own_out),
-        (wl_ref, 0, left_out),
-        (wr_ref, 0, right_out),
-    ):
-        total = None
-        for b in range(3):
-            rows = blocks[b][...]
-            weight = jnp.concatenate(
-                [weights[first + b * chunks + c : first + b * chunks + c + 1, :] for c in range(chunks)],
-                axis=1,
-            )
-            weighted = (rows[:members].astype(F32) * weight).astype(BF16)
-            term = dot_nt(weighted, rows)
-            total = term if total is None else total + term
-        out[...] = total
+        pert_ref[:members, lanes] = (part - mean).astype(BF16)
 
 
 def update_kernel(members, tiles, g_ref, gl_ref, gr_ref, mean_ref, pert_ref, out_ref, wide):
-    total = g_ref[...] + (gl_ref[...] + gr_ref[...])
-    row = lax.broadcasted_iota(jnp.int32, (members, members), 0)
-    col = lax.broadcasted_iota(jnp.int32, (members, members), 1)
-    diagonal = row == col
-    gram = total[:, :members] + jnp.where(diagonal, (members - 1) / INFLATION, 0.0)
-    tail = total.shape[1] - LANES
-    drive = total[:, tail:]
+    gram, drive = unpacked_gram(members, g_ref[...] + (gl_ref[...] + gr_ref[...]))
+    size = gram.shape[0]
+    row = lax.broadcasted_iota(jnp.int32, (size, size), 0)
+    col = lax.broadcasted_iota(jnp.int32, (size, size), 1)
+    diagonal = (row == col) & (row < members)
+    gram = gram + jnp.where(diagonal, (members - 1) / INFLATION, 0.0)
     square = jnp.sum(jnp.sum(gram * gram, axis=1, keepdims=True), axis=0, keepdims=True)
     norm = jnp.sqrt(square)
 
@@ -164,20 +228,20 @@
 
     current = gram / norm
     correction = correction_of(current)
-    inverse = correction
+    moved = jnp.sum(correction * drive, axis=1, keepdims=True)
+    inverse = jnp.where(col == members, moved, correction)
     for step in range(1, NS_STEPS + 1):
         m = halves(correction)
         if step > 1:
             inverse = product(m, halves(inverse))
         if step == NS_STEPS:
             break
-        current = product(halves(current), m)
-        correction = correction_of(product(halves(inverse), halves(current)))
-    root = halves(inverse)
-    shift = product(root, halves(product(root, halves(drive))))
-    shift = shift[:, members - tail : members - tail + 1]
-    weights = (math.sqrt(members - 1) / jnp.sqrt(norm) * inverse + shift / norm).astype(BF16)
-    update = dot_tn(weights, pert_ref[...])
+        current = product(halves(product(halves(current), m)), m)
+        correction = correction_of(current)
+    shift = jnp.sum(inverse * inverse[:, members : members + 1], axis=0, keepdims=True)
+    weights = math.sqrt(members - 1) / jnp.sqrt(norm) * inverse + shift / norm
+    weights = weights[:members].astype(BF16)
+    update = dot_nn(weights, pert_ref[...])
     for t in range(tiles):
         lanes = slice(t * LANES, (t + 1) * LANES)
         wide[pl.ds(t, members, stride=tiles), :] = mean_ref[:, lanes] + update[:, lanes]
@@ -216,7 +280,16 @@
     packed = call(
         functools.partial(pack_kernel, regions, tiles),
         jax.ShapeDtypeStruct((regions, rows, LANES), BF16),
-        [pltpu.VMEM((regions * rows, LANES), F32)],
+        [
+            pltpu.VMEM((share, regions * cells), BF16),
+            pltpu.VMEM((regions * rows, LANES), F32),
+            pltpu.VMEM((regions, rows, LANES), BF16),
+            pltpu.SemaphoreType.DMA((PIECES,)),
+            pltpu.SemaphoreType.DMA((PIECES,)),
+        ],
+        in_specs=[pl.BlockSpec(memory_space=pl.ANY)],
+        out_specs=pl.BlockSpec(memory_space=pl.ANY),
+        limit=PACK_LIMIT,
         nbytes=2 * 2 * share * regions * cells,
     )(background.reshape(share, regions * cells))
     state = lax.all_to_all(packed, "mem", split_axis=0, concat_axis=0, tiled=True)
@@ -231,28 +304,29 @@
         wide,
         flops=2 * members * cells * width,
         nbytes=2 * members * cells,
-    )(state, index, yobs[0])
+    )(state, index, yobs[0], weight_left, weight_right)
     before = lax.ppermute(observed, "mem", mem_up)
     after = lax.ppermute(observed, "mem", mem_down)
-    mean, pert = call(
-        functools.partial(state_kernel, tiles),
+    gram_shape = jax.ShapeDtypeStruct((2 * LANES, LANES), F32)
+    to_left, to_right = call(
+        functools.partial(neighbour_kernel, members),
+        (gram_shape,) * 2,
+        flops=12 * members * padded * width,
+        nbytes=8 * members * padded,
+    )(before, observed, after, weight_left, weight_right)
+    gram_a = lax.ppermute(to_left, "reg", reg_down)
+    gram_b = lax.ppermute(to_right, "reg", reg_up)
+    gram, mean, pert = call(
+        functools.partial(own_kernel, members, tiles),
         (
+            gram_shape,
             jax.ShapeDtypeStruct((1, cells), F32),
-            jax.ShapeDtypeStruct((members, cells), BF16),
+            jax.ShapeDtypeStruct((padded, cells), BF16),
         ),
         wide,
-        flops=4 * members * cells,
-        nbytes=4 * members * cells,
-    )(state)
-    gram_shape = jax.ShapeDtypeStruct((members, padded), F32)
-    gram, to_left, to_right = call(
-        functools.partial(gram_kernel, members),
-        (gram_shape,) * 3,
-        flops=18 * members * padded * width,
-        nbytes=12 * members * padded,
-    )(before, observed, after, weight, weight_left, weight_right)
-    gram_a = lax.ppermute(to_left, "reg", reg_down)
-    gram_b = lax.ppermute(to_right, "reg", reg_up)
+        flops=6 * members * padded * width,
+        nbytes=8 * members * cells,
+    )(before, observed, after, weight, state)
     analysis = call(
         functools.partial(update_kernel, members, tiles),
         jax.ShapeDtypeStruct((members * tiles, LANES), BF16),
@@ -266,7 +340,12 @@
     out = call(
         functools.partial(unpack_kernel, regions, tiles),
         jax.ShapeDtypeStruct((share, regions * cells), BF16),
-        [pltpu.VMEM((regions * rows, LANES), F32)],
+        [
+            pltpu.VMEM((regions * rows, LANES), F32),
+            pltpu.VMEM((share, regions * cells), BF16),
+            pltpu.SemaphoreType.DMA((PIECES,)),
+        ],
+        out_specs=pl.BlockSpec(memory_space=pl.ANY),
         nbytes=2 * 2 * share * regions * cells,
     )(returned)
     return out.reshape(share, 1, regions * cells)

time: 108 us -> 100 us (0.926)
  waiting for transfers between devices: 30.1 us -> 20.5 us
  blocking collectives: 29.7 us -> 31.3 us
  local copies, waits for them, and re-layouts: 1.17 us -> 0.04 us
    all_to_all x1, waiting for transfers between devices: 21.4 us -> 4.73 us  [local(): lax.all_to_all(packed, 'mem', split_axis=0, concat_axis=0, tiled=True)]
    ppermute x1, waiting for transfers between devices: 0.01 us -> 6.02 us  [local(): weight_left = lax.ppermute(weight[6 * chunks:], 'reg', reg_up)]
    ppermute x1, waiting for transfers between devices: 0.01 us -> 3.18 us  [local(): after = lax.ppermute(observed, 'mem', mem_down)]
    all_to_all x1, blocking collectives: 29.7 us -> 31.3 us  [local(): lax.all_to_all(analysis.reshape(regions, rows, LANES), 'mem', split_axis=...]
    ppermute x1, starting transfers between devices: 6.01 us -> 7.29 us  [local(): weight_right = lax.ppermute(weight[:3 * chunks], 'reg', reg_down)]
    ppermute x1, starting transfers between devices: 3.2 us -> 1.92 us  [local(): weight_left = lax.ppermute(weight[6 * chunks:], 'reg', reg_up)]
    unnamed x10 -> x8, local copies, waits for them, and re-layouts: 1.16 us -> 0.02 us
  transfers between devices with their start and end apart: 7 -> 7, of which waited for: 4 -> 5; matrix products, arithmetic and copies ran while one was open for 0% -> 0% of each run, Pallas kernels for 1% -> 1%
where the time goes in v2:
time: 100 us; the launch traced here: 99.7 us
  starting transfers between devices  37.7 us (38%)
  blocking collectives  31.3 us (31%)
  waiting for transfers between devices  20.5 us (20%)
  Pallas kernels  9.27 us (9%)
    all_to_all x1, blocking collectives, local(): lax.all_to_all(analysis.reshape(regions, rows, LANES), 'mem', split_axis=...  31.3 us
    all_to_all x1, starting transfers between devices, local(): lax.all_to_all(packed, 'mem', split_axis=0, concat_axis=0, tiled=True)  16.7 us
    ppermute x1, starting transfers between devices, local(): weight_right = lax.ppermute(weight[:3 * chunks], 'reg', reg_down)  7.29 us
    ppermute x1, starting transfers between devices, local(): gram_a = lax.ppermute(to_left, 'reg', reg_down)  7.28 us
    ppermute x1, waiting for transfers between devices, local(): gram_b = lax.ppermute(to_right, 'reg', reg_up)  6.44 us
    ppermute x1, waiting for transfers between devices, local(): weight_left = lax.ppermute(weight[6 * chunks:], 'reg', reg_up)  6.02 us
    all_to_all x1, waiting for transfers between devices, local(): lax.all_to_all(packed, 'mem', split_axis=0, concat_axis=0, tiled=True)  4.73 us
    pallas_call x1, Pallas kernels, local(): call(functools.partial(update_kernel, members, tiles), jax.ShapeDtypeStru...  3.43 us
  transfers between devices with their start and end apart: 7, of which 5 were waited for; matrix products, arithmetic and copies ran while one was open for 0% of the time, Pallas kernels for 1%

profile of v2, /device:TPU:1, one launch (start us, length us, event | category | flops | bytes accessed | tf_op | source)
XLA Modules:
  0.0 99.7 jit_solution(5603795232513229987)
XLA Ops:
  0.0 0.0 copy-start
  0.0 2.0 %shard_map.64 = bf16[24,80,128]{2,1,0:T(8,128)(2,1)} custom-call(bf16[10,24576]{1,0:T(8,128)(2,1)} %bitcast.15), custom_call_target="tpu_custom_call" | custom-call | bytes 983040 | tf_op jit(solution)/shard_map/pallas_call | solution.py:280
  2.0 0.0 copy-start.1
  2.0 0.0 copy-start.2
  2.0 16.7 %all-to-all-start = ((bf16[24,80,128]{2,1,0:T(8,128)(2,1)}), bf16[24,80,128]{2,1,0:T(8,128)(2,1)S(1)}, u32[]{:S(2)}, u32[]{:S(2)}) async-start(bf16[24,80,128]{2,1,0:T(8,128)(2,1)} %shard_map.64), calls=%async_computation | async-start | bytes 983040 | tf_op jit(solution)/shard_map/all_to_all | solution.py:295
  19.4 0.0 copy-done.1
  19.4 0.0 copy-done.2
  19.4 0.7 shard_map.65.w_ref
  20.1 7.3 %collective-permute-start.1 = (f32[12,128]{1,0:T(8,128)S(1)}, f32[12,128]{1,0:T(8,128)S(1)}, u32[]{:S(2)}, u32[]{:S(2)}) collective-permute-start(f32[12,128]{1,0:T(8,128)S(1)} %get-tuple-element.15), channel_id=1, source_target_pairs={{1,0},{2,1},{3,2},{4,3},{5,4},{6,5},{7,6},{8,7},{9,8},{10,9},{11,1... | collective-permute-start | bytes 18440 | tf_op jit(solution)/shard_map/ppermute | solution.py:277
  27.4 1.9 %collective-permute-start = (f32[12,128]{1,0:T(8,128)S(1)}, f32[12,128]{1,0:T(8,128)S(1)}, u32[]{:S(2)}, u32[]{:S(2)}) collective-permute-start(f32[12,128]{1,0:T(8,128)S(1)} %get-tuple-element.16), channel_id=1, source_target_pairs={{0,1},{1,2},{2,3},{3,4},{4,5},{5,6},{6,7},{7,8},{8,9},{9,10},{10,1... | collective-permute-start | bytes 18440 | tf_op jit(solution)/shard_map/ppermute | solution.py:278
  29.4 0.0 copy-done
  29.4 0.0 copy-start.3
  29.4 0.0 collective-permute-done.1.wr_ref
  29.4 6.0 %collective-permute-done.wl_ref = f32[12,128]{1,0:T(8,128)S(1)} collective-permute-done((f32[12,128]{1,0:T(8,128)S(1)}, f32[12,128]{1,0:T(8,128)S(1)}, u32[]{:S(2)}, u32[]{:S(2)}) %collective-permute-start) | collective-permute-done | bytes 6176 | tf_op jit(solution)/shard_map/ppermute | solution.py:278
  35.4 4.7 %all-to-all-done = bf16[24,80,128]{2,1,0:T(8,128)(2,1)S(1)} async-done(((bf16[24,80,128]{2,1,0:T(8,128)(2,1)}), bf16[24,80,128]{2,1,0:T(8,128)(2,1)S(1)}, u32[]{:S(2)}, u32[]{:S(2)}) %all-to-all-start) | async-done | bytes 491552 | tf_op jit(solution)/shard_map/all_to_all | solution.py:295
  40.2 0.0 copy-done.3
  40.2 0.8 shard_map.66.own_ref
  40.9 2.6 %collective-permute-start.3 = (bf16[256,512]{1,0:T(8,128)(2,1)S(1)}, bf16[256,512]{1,0:T(8,128)(2,1)S(1)}, u32[]{:S(2)}, u32[]{:S(2)}) collective-permute-start(bf16[256,512]{1,0:T(8,128)(2,1)S(1)} %shard_map.66.own_ref), channel_id=1, source_target_pairs={{32,0},{64,32},{96,64},{128,96},{160,128},{192,160},{224,192},{256... | collective-permute-start | bytes 786440 | tf_op jit(solution)/shard_map/ppermute | solution.py:309
  43.6 0.0 collective-permute-start.2
  43.6 3.2 %collective-permute-done.3.after_ref = bf16[256,512]{1,0:T(8,128)(2,1)S(1)} collective-permute-done((bf16[256,512]{1,0:T(8,128)(2,1)S(1)}, bf16[256,512]{1,0:T(8,128)(2,1)S(1)}, u32[]{:S(2)}, u32[]{:S(2)}) %collective-permute-start.3) | collective-permute-done | bytes 262176 | tf_op jit(solution)/shard_map/ppermute | solution.py:309
  46.8 0.1 collective-permute-done.2.before_ref
  46.9 0.7 shard_map.68
  47.6 7.3 %collective-permute-start.4 = (f32[256,128]{1,0:T(8,128)S(1)}, f32[256,128]{1,0:T(8,128)S(1)}, u32[]{:S(2)}, u32[]{:S(2)}) collective-permute-start(f32[256,128]{1,0:T(8,128)S(1)} %get-tuple-element.11), channel_id=1, source_target_pairs={{1,0},{2,1},{3,2},{4,3},{5,4},{6,5},{7,6},{8,7},{9,8},{10,9},{11,1... | collective-permute-start | bytes 393224 | tf_op jit(solution)/shard_map/ppermute | solution.py:317
  54.9 1.9 %collective-permute-start.5 = (f32[256,128]{1,0:T(8,128)S(1)}, f32[256,128]{1,0:T(8,128)S(1)}, u32[]{:S(2)}, u32[]{:S(2)}) collective-permute-start(f32[256,128]{1,0:T(8,128)S(1)} %get-tuple-element.12), channel_id=1, source_target_pairs={{0,1},{1,2},{2,3},{3,4},{4,5},{5,6},{6,7},{7,8},{8,9},{9,10},{10,1... | collective-permute-start | bytes 393224 | tf_op jit(solution)/shard_map/ppermute | solution.py:318
  56.8 0.7 shard_map.67
  57.5 0.0 collective-permute-done.4.gl_ref
  57.5 6.4 %collective-permute-done.5.gr_ref = f32[256,128]{1,0:T(8,128)S(1)} collective-permute-done((f32[256,128]{1,0:T(8,128)S(1)}, f32[256,128]{1,0:T(8,128)S(1)}, u32[]{:S(2)}, u32[]{:S(2)}) %collective-permute-start.5) | collective-permute-done | bytes 131104 | tf_op jit(solution)/shard_map/ppermute | solution.py:318
  63.9 3.4 %shard_map.69 = bf16[1920,128]{1,0:T(8,128)(2,1)S(1)} custom-call(f32[256,128]{1,0:T(8,128)S(1)} %get-tuple-element.10.g_ref, f32[256,128]{1,0:T(8,128)S(1)} %collective-permute-done.4.gl_ref, f32[256,128]{1,0:T(8,128)S(1)} %collective-permute-done.5.gr_ref, f32[1,1024]{1,0:T(1,128)S(1)} %get-tuple-element.13.mean_ref, ...), custom_call_target="tpu_custom_call" | custom-call | flops 1223884800 | bytes 983040 | tf_op jit(solution)/shard_map/pallas_call | solution.py:330
  67.4 31.3 %all_to_all.10.x_ref = bf16[24,80,128]{2,1,0:T(8,128)(2,1)S(1)} all-to-all(bf16[24,80,128]{2,1,0:T(8,128)(2,1)S(1)} %bitcast.11), channel_id=1, replica_groups=mesh['mem'=24,'reg'=32] {'mem'}, dimensions={0} | all-to-all | bytes 983040 | tf_op jit(solution)/shard_map/all_to_all | solution.py:337
  98.7 1.0 %shard_map.70 = bf16[10,24576]{1,0:T(8,128)(2,1)} custom-call(bf16[24,80,128]{2,1,0:T(8,128)(2,1)S(1)} %all_to_all.10.x_ref), custom_call_target="tpu_custom_call" | custom-call | bytes 983040 | tf_op jit(solution)/shard_map/pallas_call | solution.py:340
  (2 shorter events, 0.0 us)
Async XLA Ops:
  0.0 29.4 %copy-start = (s32[1,24,512]{2,1,0:T(8,128)S(1)}, s32[1,24,512]{2,1,0:T(8,128)}, u32[]{:S(2)}) copy-start(s32[1,24,512]{2,1,0:T(8,128)} %param.7) | copy-start | bytes 147460
  2.0 17.4 %copy-start.1 = (s32[1,1,2048]{2,1,0:T(1,128)S(1)}, s32[1,1,2048]{2,1,0:T(1,128)}, u32[]{:S(2)}) copy-start(s32[1,1,2048]{2,1,0:T(1,128)} %param.9) | copy-start | bytes 24580
  2.0 17.4 %copy-start.2 = (f32[1,1,2048]{2,1,0:T(1,128)S(1)}, f32[1,1,2048]{2,1,0:T(1,128)}, u32[]{:S(2)}) copy-start(f32[1,1,2048]{2,1,0:T(1,128)} %param.11) | copy-start | bytes 24580
  2.0 38.1 %all-to-all-start = ((bf16[24,80,128]{2,1,0:T(8,128)(2,1)}), bf16[24,80,128]{2,1,0:T(8,128)(2,1)S(1)}, u32[]{:S(2)}, u32[]{:S(2)}) async-start(bf16[24,80,128]{2,1,0:T(8,128)(2,1)} %shard_map.64), calls=%async_computation | async-start | bytes 983040 | tf_op jit(solution)/shard_map/all_to_all | solution.py:295
  20.1 9.3 %collective-permute-start.1 = (f32[12,128]{1,0:T(8,128)S(1)}, f32[12,128]{1,0:T(8,128)S(1)}, u32[]{:S(2)}, u32[]{:S(2)}) collective-permute-start(f32[12,128]{1,0:T(8,128)S(1)} %get-tuple-element.15), channel_id=1, source_target_pairs={{1,0},{2,1},{3,2},{4,3},{5,4},{6,5},{7,6},{8,7},{9,8},{10,9},{11,1... | collective-permute-start | bytes 18440 | tf_op jit(solution)/shard_map/ppermute | solution.py:277
  27.4 8.0 %collective-permute-start = (f32[12,128]{1,0:T(8,128)S(1)}, f32[12,128]{1,0:T(8,128)S(1)}, u32[]{:S(2)}, u32[]{:S(2)}) collective-permute-start(f32[12,128]{1,0:T(8,128)S(1)} %get-tuple-element.16), channel_id=1, source_target_pairs={{0,1},{1,2},{2,3},{3,4},{4,5},{5,6},{6,7},{7,8},{8,9},{9,10},{10,1... | collective-permute-start | bytes 18440 | tf_op jit(solution)/shard_map/ppermute | solution.py:278
  29.4 10.8 %copy-start.3 = (bf16[1,1,512]{2,1,0:T(2,128)(2,1)S(1)}, bf16[1,1,512]{2,1,0:T(2,128)(2,1)}, u32[]{:S(2)}) copy-start(bf16[1,1,512]{2,1,0:T(2,128)(2,1)} %param.8) | copy-start | bytes 3076
  40.9 5.8 %collective-permute-start.3 = (bf16[256,512]{1,0:T(8,128)(2,1)S(1)}, bf16[256,512]{1,0:T(8,128)(2,1)S(1)}, u32[]{:S(2)}, u32[]{:S(2)}) collective-permute-start(bf16[256,512]{1,0:T(8,128)(2,1)S(1)} %shard_map.66.own_ref), channel_id=1, source_target_pairs={{32,0},{64,32},{96,64},{128,96},{160,128},{192,160},{224,192},{256... | collective-permute-start | bytes 786440 | tf_op jit(solution)/shard_map/ppermute | solution.py:309
  43.6 3.3 %collective-permute-start.2 = (bf16[256,512]{1,0:T(8,128)(2,1)S(1)}, bf16[256,512]{1,0:T(8,128)(2,1)S(1)}, u32[]{:S(2)}, u32[]{:S(2)}) collective-permute-start(bf16[256,512]{1,0:T(8,128)(2,1)S(1)} %shard_map.66.own_ref), channel_id=1, source_target_pairs={{0,32},{32,64},{64,96},{96,128},{128,160},{160,192},{192,224},{224... | collective-permute-start | bytes 786440 | tf_op jit(solution)/shard_map/ppermute | solution.py:308
  47.6 9.9 %collective-permute-start.4 = (f32[256,128]{1,0:T(8,128)S(1)}, f32[256,128]{1,0:T(8,128)S(1)}, u32[]{:S(2)}, u32[]{:S(2)}) collective-permute-start(f32[256,128]{1,0:T(8,128)S(1)} %get-tuple-element.11), channel_id=1, source_target_pairs={{1,0},{2,1},{3,2},{4,3},{5,4},{6,5},{7,6},{8,7},{9,8},{10,9},{11,1... | collective-permute-start | bytes 393224 | tf_op jit(solution)/shard_map/ppermute | solution.py:317
  54.9 9.0 %collective-permute-start.5 = (f32[256,128]{1,0:T(8,128)S(1)}, f32[256,128]{1,0:T(8,128)S(1)}, u32[]{:S(2)}, u32[]{:S(2)}) collective-permute-start(f32[256,128]{1,0:T(8,128)S(1)} %get-tuple-element.12), channel_id=1, source_target_pairs={{0,1},{1,2},{2,3},{3,4},{4,5},{5,6},{6,7},{7,8},{8,9},{9,10},{10,1... | collective-permute-start | bytes 393224 | tf_op jit(solution)/shard_map/ppermute | solution.py:318

commit v3 on v2

--- a/solution.py
+++ b/solution.py
@@ -28,6 +28,16 @@
         cost_estimate=pl.CostEstimate(flops=flops, bytes_accessed=nbytes, transcendentals=0),
         **specs,
     )
+
+
+SCALARS = pl.BlockSpec(memory_space=pltpu.SMEM)
+WHOLE = pl.BlockSpec(memory_space=pltpu.VMEM)
+
+
+def swap(block, axis, place):
+    size = lax.axis_size(axis)
+    pairs = [(i, (i + 1) % size) for i in range(place, size, 2)]
+    return lax.ppermute(block, axis, pairs + [(j, i) for i, j in pairs])
 
 
 def dot_nn(a, b):
@@ -104,9 +114,10 @@
         given(piece).wait()
 
 
-def weight_kernel(list_ref, count_ref, weight_ref, out_ref):
+def weight_kernel(side_ref, list_ref, count_ref, weight_ref, out_ref, odd_ref, even_ref):
     length = list_ref.shape[1]
-    rows = out_ref.shape[0]
+    third = out_ref.shape[0]
+    rows = 3 * third
     order = list_ref[...]
     position = lax.broadcasted_iota(jnp.int32, (1, length), 1)
     live = jnp.where(position < count_ref[...], weight_ref[...], 0.0)
@@ -123,10 +134,15 @@
     def spread(part):
         return dot_nt(jnp.where(at_row, part.astype(F32), 0.0).astype(BF16), lane_hot)
 
-    out_ref[...] = (spread(high) + spread(middle)) + spread(low)
-
-
-def observe_kernel(tiles, x_ref, index_ref, yobs_ref, wl_ref, wr_ref, out_ref, wide):
+    dense = (spread(high) + spread(middle)) + spread(low)
+    left, right = dense[:third], dense[2 * third :]
+    paired_left = side_ref[1] == 0
+    out_ref[...] = dense[third : 2 * third]
+    odd_ref[...] = jnp.where(paired_left, left, right)
+    even_ref[...] = jnp.where(paired_left, right, left)
+
+
+def observe_kernel(tiles, x_ref, index_ref, yobs_ref, wo_ref, we_ref, out_ref, wide):
     cells = tiles * LANES
     members = x_ref.shape[0] // tiles
     width = index_ref.shape[1]
@@ -146,13 +162,13 @@
     out_ref[members:, :] = jnp.where(row == 0, innovation, 0.0).astype(BF16)
 
 
-def packed_gram(members, blocks, w_ref, first):
-    chunks = blocks[0].shape[1] // LANES
+def packed_gram(members, side_ref, own_ref, odd_ref, even_ref, w_ref):
+    chunks = own_ref.shape[1] // LANES
+    side = side_ref[0]
     total = None
-    for b in range(3):
-        rows = blocks[b][...]
-        start = first + b * chunks
-        weight = jnp.concatenate([w_ref[start + c : start + c + 1, :] for c in range(chunks)], axis=1)
+    for rows_ref, b in ((own_ref, 1), (odd_ref, 2 * side), (even_ref, 2 - 2 * side)):
+        rows = rows_ref[...]
+        weight = jnp.concatenate([w_ref[pl.ds(b * chunks + c, 1), :] for c in range(chunks)], axis=1)
         term = dot_nt((rows[:members].astype(F32) * weight).astype(BF16), rows)
         total = term if total is None else total + term
     rest = members - LANES
@@ -194,14 +210,12 @@
     return gram, drive
 
 
-def neighbour_kernel(members, before_ref, own_ref, after_ref, wl_ref, wr_ref, left_out, right_out):
-    blocks = (before_ref, own_ref, after_ref)
-    left_out[...] = packed_gram(members, blocks, wl_ref, 0)
-    right_out[...] = packed_gram(members, blocks, wr_ref, 0)
-
-
-def own_kernel(members, tiles, before_ref, own_ref, after_ref, w_ref, x_ref, gram_out, mean_ref, pert_ref, wide):
-    gram_out[...] = packed_gram(members, (before_ref, own_ref, after_ref), w_ref, w_ref.shape[0] // 3)
+def neighbour_kernel(members, side_ref, own_ref, odd_ref, even_ref, w_ref, out_ref):
+    out_ref[...] = packed_gram(members, side_ref, own_ref, odd_ref, even_ref, w_ref)
+
+
+def own_kernel(members, tiles, side_ref, own_ref, odd_ref, even_ref, w_ref, x_ref, gram_out, mean_ref, pert_ref, wide):
+    gram_out[...] = packed_gram(members, side_ref, own_ref, odd_ref, even_ref, w_ref)
     wide[...] = x_ref[...].astype(F32)
     extra = pert_ref.shape[0] - members
     pert_ref[members:, :] = jnp.zeros((extra, pert_ref.shape[1]), BF16)
@@ -213,8 +227,8 @@
         pert_ref[:members, lanes] = (part - mean).astype(BF16)
 
 
-def update_kernel(members, tiles, g_ref, gl_ref, gr_ref, mean_ref, pert_ref, out_ref, wide):
-    gram, drive = unpacked_gram(members, g_ref[...] + (gl_ref[...] + gr_ref[...]))
+def update_kernel(members, tiles, g_ref, odd_ref, even_ref, mean_ref, pert_ref, out_ref, wide):
+    gram, drive = unpacked_gram(members, g_ref[...] + (odd_ref[...] + even_ref[...]))
     size = gram.shape[0]
     row = lax.broadcasted_iota(jnp.int32, (size, size), 0)
     col = lax.broadcasted_iota(jnp.int32, (size, size), 1)
@@ -260,22 +274,18 @@
     chunks = width // LANES
     cand_rows = 9 * chunks
 
-    def ring(axis):
-        size = lax.axis_size(axis)
-        up = [(i, (i + 1) % size) for i in range(size)]
-        return up, [(j, i) for i, j in up]
-
-    mem_up, mem_down = ring("mem")
-    reg_up, reg_down = ring("reg")
-
-    weight = call(
+    own_row = lax.axis_index("mem")
+    side = jnp.stack([own_row % 2, lax.axis_index("reg") % 2]).astype(jnp.int32)
+    weight_shape = jax.ShapeDtypeStruct((3 * chunks, LANES), F32)
+    weight, weight_odd, weight_even = call(
         weight_kernel,
-        jax.ShapeDtypeStruct((cand_rows, LANES), F32),
-        flops=2 * 3 * cand_rows * 2048 * LANES,
+        (weight_shape,) * 3,
+        flops=6 * cand_rows * loc_list.shape[2] * LANES,
         nbytes=1 << 15,
-    )(loc_list[0], loc_count, loc_weight[0])
-    weight_right = lax.ppermute(weight[: 3 * chunks], "reg", reg_down)
-    weight_left = lax.ppermute(weight[6 * chunks :], "reg", reg_up)
+        in_specs=[SCALARS] + [WHOLE] * 3,
+    )(side, loc_list[0], loc_count, loc_weight[0])
+    weight_odd = swap(weight_odd, "reg", 1)
+    weight_even = swap(weight_even, "reg", 0)
 
     packed = call(
         functools.partial(pack_kernel, regions, tiles),
@@ -295,7 +305,6 @@
     state = lax.all_to_all(packed, "mem", split_axis=0, concat_axis=0, tiled=True)
     state = state.reshape(members * tiles, LANES)
 
-    own_row = lax.axis_index("mem")
     index = lax.dynamic_slice_in_dim(obs_index[0], own_row, 1, axis=0)
     wide = [pltpu.VMEM((members * tiles, LANES), F32)]
     observed = call(
@@ -304,18 +313,22 @@
         wide,
         flops=2 * members * cells * width,
         nbytes=2 * members * cells,
-    )(state, index, yobs[0], weight_left, weight_right)
-    before = lax.ppermute(observed, "mem", mem_up)
-    after = lax.ppermute(observed, "mem", mem_down)
+    )(state, index, yobs[0], weight_odd, weight_even)
+    rows_in = (side, observed, swap(observed, "mem", 1), swap(observed, "mem", 0))
     gram_shape = jax.ShapeDtypeStruct((2 * LANES, LANES), F32)
-    to_left, to_right = call(
-        functools.partial(neighbour_kernel, members),
-        (gram_shape,) * 2,
-        flops=12 * members * padded * width,
-        nbytes=8 * members * padded,
-    )(before, observed, after, weight_left, weight_right)
-    gram_a = lax.ppermute(to_left, "reg", reg_down)
-    gram_b = lax.ppermute(to_right, "reg", reg_up)
+
+    def to_neighbour(place, weights):
+        partial = call(
+            functools.partial(neighbour_kernel, members),
+            gram_shape,
+            flops=6 * members * padded * width,
+            nbytes=8 * members * padded,
+            in_specs=[SCALARS] + [WHOLE] * 4,
+        )(*rows_in, weights)
+        return swap(partial, "reg", place)
+
+    odd_gram = to_neighbour(1, weight_odd)
+    even_gram = to_neighbour(0, weight_even)
     gram, mean, pert = call(
         functools.partial(own_kernel, members, tiles),
         (
@@ -326,14 +339,15 @@
         wide,
         flops=6 * members * padded * width,
         nbytes=8 * members * cells,
-    )(before, observed, after, weight, state)
+        in_specs=[SCALARS] + [WHOLE] * 5,
+    )(*rows_in, weight, state)
     analysis = call(
         functools.partial(update_kernel, members, tiles),
         jax.ShapeDtypeStruct((members * tiles, LANES), BF16),
         wide,
         flops=2 * members * members * (cells + 40 * members),
         nbytes=4 * members * cells,
-    )(gram, gram_a, gram_b, mean, pert)
+    )(gram, odd_gram, even_gram, mean, pert)
     returned = lax.all_to_all(
         analysis.reshape(regions, rows, LANES), "mem", split_axis=0, concat_axis=0, tiled=True
     )

time: 100 us -> 97.9 us (0.979)
  waiting for transfers between devices: 20.5 us -> 13.4 us
  starting transfers between devices: 37.7 us -> 41.5 us
  Pallas kernels: 9.27 us -> 11.7 us
  blocking collectives: 31.3 us -> 29.2 us
    ppermute x6, waiting for transfers between devices: 15.8 us -> 6.54 us  [swap(): return lax.ppermute(block, axis, pairs + [(j, i) for i, j in pairs])]
    ppermute x6, starting transfers between devices: 21 us -> 24.8 us  [swap(): return lax.ppermute(block, axis, pairs + [(j, i) for i, j in pairs])]
    all_to_all x1, blocking collectives: 31.3 us -> 29.2 us  [local(): lax.all_to_all(analysis.reshape(regions, rows, LANES), 'mem', split_axis=...]
    all_to_all x1, waiting for transfers between devices: 4.73 us -> 6.81 us  [local(): lax.all_to_all(packed, 'mem', split_axis=0, concat_axis=0, tiled=True)]
    pallas_call x2 -> x3, Pallas kernels: 1.42 us -> 3.31 us  [the longest x2 2.06 us: to_neighbour(): call(functools.partial(neighbour_kernel, members), gram_shape, flops=6 *...]
  transfers between devices with their start and end apart: 7 -> 7, of which waited for: 5 -> 4; matrix products, arithmetic and copies ran while one was open for 0% -> 0% of each run, Pallas kernels for 1% -> 4%
where the time goes in v3:
time: 97.9 us; the launch traced here: 97.4 us
  starting transfers between devices  41.5 us (42%)
  blocking collectives  29.2 us (30%)
  waiting for transfers between devices  13.4 us (14%)
  Pallas kernels  11.7 us (12%)
    all_to_all x1, blocking collectives, local(): lax.all_to_all(analysis.reshape(regions, rows, LANES), 'mem', split_axis=...  29.2 us
    ppermute x6, starting transfers between devices, swap(): return lax.ppermute(block, axis, pairs + [(j, i) for i, j in pairs])  24.8 us
    all_to_all x1, starting transfers between devices, local(): lax.all_to_all(packed, 'mem', split_axis=0, concat_axis=0, tiled=True)  16.7 us
    all_to_all x1, waiting for transfers between devices, local(): lax.all_to_all(packed, 'mem', split_axis=0, concat_axis=0, tiled=True)  6.81 us
    ppermute x6, waiting for transfers between devices, swap(): return lax.ppermute(block, axis, pairs + [(j, i) for i, j in pairs])  6.54 us
    pallas_call x1, Pallas kernels, local(): call(functools.partial(update_kernel, members, tiles), jax.ShapeDtypeStru...  3.43 us
    pallas_call x2, Pallas kernels, to_neighbour(): call(functools.partial(neighbour_kernel, members), gram_shape, flops=6 *...  2.06 us
    pallas_call x1, Pallas kernels, local(): call(functools.partial(pack_kernel, regions, tiles), jax.ShapeDtypeStruct...  2 us
  transfers between devices with their start and end apart: 7, of which 4 were waited for; matrix products, arithmetic and copies ran while one was open for 0% of the time, Pallas kernels for 4%

profile of v3, /device:TPU:1, one launch (start us, length us, event | category | flops | bytes accessed | tf_op | source)
XLA Modules:
  0.0 97.4 jit_solution(2295328861272938934)
XLA Ops:
  0.0 0.0 copy-start
  0.0 2.0 %shard_map.64 = bf16[24,80,128]{2,1,0:T(8,128)(2,1)} custom-call(bf16[10,24576]{1,0:T(8,128)(2,1)} %bitcast.17), custom_call_target="tpu_custom_call" | custom-call | bytes 983040 | tf_op jit(solution)/shard_map/pallas_call | solution.py:290
  2.0 16.7 %all-to-all-start = ((bf16[24,80,128]{2,1,0:T(8,128)(2,1)}), bf16[24,80,128]{2,1,0:T(8,128)(2,1)S(1)}, u32[]{:S(2)}, u32[]{:S(2)}) async-start(bf16[24,80,128]{2,1,0:T(8,128)(2,1)} %shard_map.64), calls=%async_computation | async-start | bytes 983040 | tf_op jit(solution)/shard_map/all_to_all | solution.py:305
  19.4 0.0 copy-start.2
  19.4 0.0 copy-start.1
  19.4 0.1 pad_add_fusion.side_ref
  19.5 0.6 copy-done.2
  20.1 0.0 copy-done.1
  20.1 1.3 %shard_map.65 = (f32[12,128]{1,0:T(8,128)S(1)}, f32[12,128]{1,0:T(8,128)S(1)}, f32[12,128]{1,0:T(8,128)S(1)}) custom-call(s32[2]{0:T(128)S(1)} %pad_add_fusion.side_ref, s32[1,2048]{1,0:T(1,128)S(1)} %bitcast.14, s32[1,1]{1,0:T(1,128)S(6)} %copy.7.count_ref, f32[1,2048]{1,0:T(1,128)S(1)} %bitcast.15), custom_call_target="tpu_custom_call" | custom-call | flops 56623104 | bytes 32768 | tf_op jit(solution)/shard_map/pallas_call | solution.py:280
  21.4 7.3 %collective-permute-start = (f32[12,128]{1,0:T(8,128)S(1)}, f32[12,128]{1,0:T(8,128)S(1)}, u32[]{:S(2)}, u32[]{:S(2)}) collective-permute-start(f32[12,128]{1,0:T(8,128)S(1)} %get-tuple-element.11), channel_id=1, source_target_pairs={{1,2},{3,4},{5,6},{7,8},{9,10},{11,12},{13,14},{15,16},{17,18},{19... | collective-permute-start | bytes 18440 | tf_op jit(solution)/shard_map/ppermute | solution.py:40
  28.7 1.9 %collective-permute-start.1 = (f32[12,128]{1,0:T(8,128)S(1)}, f32[12,128]{1,0:T(8,128)S(1)}, u32[]{:S(2)}, u32[]{:S(2)}) collective-permute-start(f32[12,128]{1,0:T(8,128)S(1)} %get-tuple-element.12), channel_id=1, source_target_pairs={{0,1},{2,3},{4,5},{6,7},{8,9},{10,11},{12,13},{14,15},{16,17},{18,... | collective-permute-start | bytes 18440 | tf_op jit(solution)/shard_map/ppermute | solution.py:40
  30.6 0.0 copy-done
  30.6 0.0 copy-start.3
  30.6 0.0 collective-permute-done.wo_ref.w_ref
  30.6 2.7 %collective-permute-done.1.we_ref.w_ref = f32[12,128]{1,0:T(8,128)S(1)} collective-permute-done((f32[12,128]{1,0:T(8,128)S(1)}, f32[12,128]{1,0:T(8,128)S(1)}, u32[]{:S(2)}, u32[]{:S(2)}) %collective-permute-start.1) | collective-permute-done | bytes 6176 | tf_op jit(solution)/shard_map/ppermute | solution.py:40
  33.3 6.8 %all-to-all-done = bf16[24,80,128]{2,1,0:T(8,128)(2,1)S(1)} async-done(((bf16[24,80,128]{2,1,0:T(8,128)(2,1)}), bf16[24,80,128]{2,1,0:T(8,128)(2,1)S(1)}, u32[]{:S(2)}, u32[]{:S(2)}) %all-to-all-start) | async-done | bytes 491552 | tf_op jit(solution)/shard_map/all_to_all | solution.py:305
  40.2 0.0 copy-done.3
  40.2 0.8 shard_map.66.own_ref
  40.9 2.2 %collective-permute-start.2 = (bf16[256,512]{1,0:T(8,128)(2,1)S(1)}, bf16[256,512]{1,0:T(8,128)(2,1)S(1)}, u32[]{:S(2)}, u32[]{:S(2)}) collective-permute-start(bf16[256,512]{1,0:T(8,128)(2,1)S(1)} %shard_map.66.own_ref), channel_id=1, source_target_pairs={{32,64},{96,128},{160,192},{224,256},{288,320},{352,384},{416,448}... | collective-permute-start | bytes 786440 | tf_op jit(solution)/shard_map/ppermute | solution.py:40
  43.1 4.3 %collective-permute-start.3 = (bf16[256,512]{1,0:T(8,128)(2,1)S(1)}, bf16[256,512]{1,0:T(8,128)(2,1)S(1)}, u32[]{:S(2)}, u32[]{:S(2)}) collective-permute-start(bf16[256,512]{1,0:T(8,128)(2,1)S(1)} %shard_map.66.own_ref), channel_id=1, source_target_pairs={{0,32},{64,96},{128,160},{192,224},{256,288},{320,352},{384,416},{... | collective-permute-start | bytes 786440 | tf_op jit(solution)/shard_map/ppermute | solution.py:40
  47.4 1.3 %collective-permute-done.2.odd_ref = bf16[256,512]{1,0:T(8,128)(2,1)S(1)} collective-permute-done((bf16[256,512]{1,0:T(8,128)(2,1)S(1)}, bf16[256,512]{1,0:T(8,128)(2,1)S(1)}, u32[]{:S(2)}, u32[]{:S(2)}) %collective-permute-start.2) | collective-permute-done | bytes 262176 | tf_op jit(solution)/shard_map/ppermute | solution.py:40
  48.6 0.0 collective-permute-done.3.even_ref
  48.6 1.0 %shard_map.68 = f32[256,128]{1,0:T(8,128)S(1)} custom-call(s32[2]{0:T(128)S(1)} %pad_add_fusion.side_ref, bf16[256,512]{1,0:T(8,128)(2,1)S(1)} %shard_map.66.own_ref, bf16[256,512]{1,0:T(8,128)(2,1)S(1)} %collective-permute-done.2.odd_ref, bf16[256,512]{1,0:T(8,128)(2,1)S(1)} %collective-permute-done.3.even_ref, f32[12,128]{1,0:T(8,128)S(1)} %collective-permute-done.wo_ref.w_ref), custom_call_target="tpu_custom_call" | custom-call | flops 188743680 | bytes 491520 | tf_op jit(solution)/shard_map/pallas_call | solution.py:321
  49.7 7.3 %collective-permute-start.4 = (f32[256,128]{1,0:T(8,128)S(1)}, f32[256,128]{1,0:T(8,128)S(1)}, u32[]{:S(2)}, u32[]{:S(2)}) collective-permute-start(f32[256,128]{1,0:T(8,128)S(1)} %shard_map.68), channel_id=1, source_target_pairs={{1,2},{3,4},{5,6},{7,8},{9,10},{11,12},{13,14},{15,16},{17,18},{19... | collective-permute-start | bytes 393224 | tf_op jit(solution)/shard_map/ppermute | solution.py:40
  56.9 1.0 %shard_map.69 = f32[256,128]{1,0:T(8,128)S(1)} custom-call(s32[2]{0:T(128)S(1)} %pad_add_fusion.side_ref, bf16[256,512]{1,0:T(8,128)(2,1)S(1)} %shard_map.66.own_ref, bf16[256,512]{1,0:T(8,128)(2,1)S(1)} %collective-permute-done.2.odd_ref, bf16[256,512]{1,0:T(8,128)(2,1)S(1)} %collective-permute-done.3.even_ref, ...), custom_call_target="tpu_custom_call" | custom-call | flops 188743680 | bytes 491520 | tf_op jit(solution)/shard_map/pallas_call | solution.py:321
  58.0 1.9 %collective-permute-start.5 = (f32[256,128]{1,0:T(8,128)S(1)}, f32[256,128]{1,0:T(8,128)S(1)}, u32[]{:S(2)}, u32[]{:S(2)}) collective-permute-start(f32[256,128]{1,0:T(8,128)S(1)} %shard_map.69), channel_id=1, source_target_pairs={{0,1},{2,3},{4,5},{6,7},{8,9},{10,11},{12,13},{14,15},{16,17},{18,... | collective-permute-start | bytes 393224 | tf_op jit(solution)/shard_map/ppermute | solution.py:40
  59.9 1.2 %shard_map.67 = (f32[256,128]{1,0:T(8,128)S(1)}, f32[1,1024]{1,0:T(1,128)S(1)}, bf16[256,1024]{1,0:T(8,128)(2,1)S(1)}) custom-call(s32[2]{0:T(128)S(1)} %pad_add_fusion.side_ref, bf16[256,512]{1,0:T(8,128)(2,1)S(1)} %shard_map.66.own_ref, bf16[256,512]{1,0:T(8,128)(2,1)S(1)} %collective-permute-done.2.odd_ref, ...), custom_call_target="tpu_custom_call" | custom-call | flops 188743680 | bytes 1966080 | tf_op jit(solution)/shard_map/pallas_call | solution.py:332
  61.1 0.0 collective-permute-done.4.odd_ref
  61.1 2.6 %collective-permute-done.5.even_ref = f32[256,128]{1,0:T(8,128)S(1)} collective-permute-done((f32[256,128]{1,0:T(8,128)S(1)}, f32[256,128]{1,0:T(8,128)S(1)}, u32[]{:S(2)}, u32[]{:S(2)}) %collective-permute-start.5) | collective-permute-done | bytes 131104 | tf_op jit(solution)/shard_map/ppermute | solution.py:40
  63.7 3.4 %shard_map.70 = bf16[1920,128]{1,0:T(8,128)(2,1)S(1)} custom-call(f32[256,128]{1,0:T(8,128)S(1)} %get-tuple-element.14.g_ref, f32[256,128]{1,0:T(8,128)S(1)} %collective-permute-done.4.odd_ref, f32[256,128]{1,0:T(8,128)S(1)} %collective-permute-done.5.even_ref, f32[1,1024]{1,0:T(1,128)S(1)} %get-tuple-element.15.mean_ref, ...), custom_call_target="tpu_custom_call" | custom-call | flops 1223884800 | bytes 983040 | tf_op jit(solution)/shard_map/pallas_call | solution.py:344
  67.1 29.2 %all_to_all.10.x_ref = bf16[24,80,128]{2,1,0:T(8,128)(2,1)S(1)} all-to-all(bf16[24,80,128]{2,1,0:T(8,128)(2,1)S(1)} %bitcast.13), channel_id=1, replica_groups=mesh['mem'=24,'reg'=32] {'mem'}, dimensions={0} | all-to-all | bytes 983040 | tf_op jit(solution)/shard_map/all_to_all | solution.py:351
  96.3 1.0 %shard_map.71 = bf16[10,24576]{1,0:T(8,128)(2,1)} custom-call(bf16[24,80,128]{2,1,0:T(8,128)(2,1)S(1)} %all_to_all.10.x_ref), custom_call_target="tpu_custom_call" | custom-call | bytes 983040 | tf_op jit(solution)/shard_map/pallas_call | solution.py:354
  (1 shorter events, 0.0 us)
Async XLA Ops:
  0.0 30.6 %copy-start = (s32[1,24,512]{2,1,0:T(8,128)S(1)}, s32[1,24,512]{2,1,0:T(8,128)}, u32[]{:S(2)}) copy-start(s32[1,24,512]{2,1,0:T(8,128)} %param.7) | copy-start | bytes 147460
  2.0 38.1 %all-to-all-start = ((bf16[24,80,128]{2,1,0:T(8,128)(2,1)}), bf16[24,80,128]{2,1,0:T(8,128)(2,1)S(1)}, u32[]{:S(2)}, u32[]{:S(2)}) async-start(bf16[24,80,128]{2,1,0:T(8,128)(2,1)} %shard_map.64), calls=%async_computation | async-start | bytes 983040 | tf_op jit(solution)/shard_map/all_to_all | solution.py:305
  19.4 0.7 copy-start.2
  19.4 0.7 copy-start.1
  21.4 9.3 %collective-permute-start = (f32[12,128]{1,0:T(8,128)S(1)}, f32[12,128]{1,0:T(8,128)S(1)}, u32[]{:S(2)}, u32[]{:S(2)}) collective-permute-start(f32[12,128]{1,0:T(8,128)S(1)} %get-tuple-element.11), channel_id=1, source_target_pairs={{1,2},{3,4},{5,6},{7,8},{9,10},{11,12},{13,14},{15,16},{17,18},{19... | collective-permute-start | bytes 18440 | tf_op jit(solution)/shard_map/ppermute | solution.py:40
  28.7 4.7 %collective-permute-start.1 = (f32[12,128]{1,0:T(8,128)S(1)}, f32[12,128]{1,0:T(8,128)S(1)}, u32[]{:S(2)}, u32[]{:S(2)}) collective-permute-start(f32[12,128]{1,0:T(8,128)S(1)} %get-tuple-element.12), channel_id=1, source_target_pairs={{0,1},{2,3},{4,5},{6,7},{8,9},{10,11},{12,13},{14,15},{16,17},{18,... | collective-permute-start | bytes 18440 | tf_op jit(solution)/shard_map/ppermute | solution.py:40
  30.6 9.5 %copy-start.3 = (bf16[1,1,512]{2,1,0:T(2,128)(2,1)S(1)}, bf16[1,1,512]{2,1,0:T(2,128)(2,1)}, u32[]{:S(2)}) copy-start(bf16[1,1,512]{2,1,0:T(2,128)(2,1)} %param.8) | copy-start | bytes 3076
  40.9 7.7 %collective-permute-start.2 = (bf16[256,512]{1,0:T(8,128)(2,1)S(1)}, bf16[256,512]{1,0:T(8,128)(2,1)S(1)}, u32[]{:S(2)}, u32[]{:S(2)}) collective-permute-start(bf16[256,512]{1,0:T(8,128)(2,1)S(1)} %shard_map.66.own_ref), channel_id=1, source_target_pairs={{32,64},{96,128},{160,192},{224,256},{288,320},{352,384},{416,448}... | collective-permute-start | bytes 786440 | tf_op jit(solution)/shard_map/ppermute | solution.py:40
  43.1 5.5 %collective-permute-start.3 = (bf16[256,512]{1,0:T(8,128)(2,1)S(1)}, bf16[256,512]{1,0:T(8,128)(2,1)S(1)}, u32[]{:S(2)}, u32[]{:S(2)}) collective-permute-start(bf16[256,512]{1,0:T(8,128)(2,1)S(1)} %shard_map.66.own_ref), channel_id=1, source_target_pairs={{0,32},{64,96},{128,160},{192,224},{256,288},{320,352},{384,416},{... | collective-permute-start | bytes 786440 | tf_op jit(solution)/shard_map/ppermute | solution.py:40
  49.7 11.5 %collective-permute-start.4 = (f32[256,128]{1,0:T(8,128)S(1)}, f32[256,128]{1,0:T(8,128)S(1)}, u32[]{:S(2)}, u32[]{:S(2)}) collective-permute-start(f32[256,128]{1,0:T(8,128)S(1)} %shard_map.68), channel_id=1, source_target_pairs={{1,2},{3,4},{5,6},{7,8},{9,10},{11,12},{13,14},{15,16},{17,18},{19... | collective-permute-start | bytes 393224 | tf_op jit(solution)/shard_map/ppermute | solution.py:40
  58.0 5.7 %collective-permute-start.5 = (f32[256,128]{1,0:T(8,128)S(1)}, f32[256,128]{1,0:T(8,128)S(1)}, u32[]{:S(2)}, u32[]{:S(2)}) collective-permute-start(f32[256,128]{1,0:T(8,128)S(1)} %shard_map.69), channel_id=1, source_target_pairs={{0,1},{2,3},{4,5},{6,7},{8,9},{10,11},{12,13},{14,15},{16,17},{18,... | collective-permute-start | bytes 393224 | tf_op jit(solution)/shard_map/ppermute | solution.py:40

commit v4 on v3

--- a/solution.py
+++ b/solution.py
@@ -136,7 +136,7 @@
 
     dense = (spread(high) + spread(middle)) + spread(low)
     left, right = dense[:third], dense[2 * third :]
-    paired_left = side_ref[1] == 0
+    paired_left = side_ref[0] == 0
     out_ref[...] = dense[third : 2 * third]
     odd_ref[...] = jnp.where(paired_left, left, right)
     even_ref[...] = jnp.where(paired_left, right, left)
@@ -162,13 +162,13 @@
     out_ref[members:, :] = jnp.where(row == 0, innovation, 0.0).astype(BF16)
 
 
-def packed_gram(members, side_ref, own_ref, odd_ref, even_ref, w_ref):
-    chunks = own_ref.shape[1] // LANES
-    side = side_ref[0]
+def packed_gram(members, blocks, w_ref):
+    chunks = blocks[0].shape[1] // LANES
     total = None
-    for rows_ref, b in ((own_ref, 1), (odd_ref, 2 * side), (even_ref, 2 - 2 * side)):
-        rows = rows_ref[...]
-        weight = jnp.concatenate([w_ref[pl.ds(b * chunks + c, 1), :] for c in range(chunks)], axis=1)
+    for b in range(3):
+        rows = blocks[b][...]
+        start = b * chunks
+        weight = jnp.concatenate([w_ref[start + c : start + c + 1, :] for c in range(chunks)], axis=1)
         term = dot_nt((rows[:members].astype(F32) * weight).astype(BF16), rows)
         total = term if total is None else total + term
     rest = members - LANES
@@ -210,12 +210,14 @@
     return gram, drive
 
 
-def neighbour_kernel(members, side_ref, own_ref, odd_ref, even_ref, w_ref, out_ref):
-    out_ref[...] = packed_gram(members, side_ref, own_ref, odd_ref, even_ref, w_ref)
-
-
-def own_kernel(members, tiles, side_ref, own_ref, odd_ref, even_ref, w_ref, x_ref, gram_out, mean_ref, pert_ref, wide):
-    gram_out[...] = packed_gram(members, side_ref, own_ref, odd_ref, even_ref, w_ref)
+def neighbour_kernel(members, before_ref, own_ref, after_ref, wo_ref, we_ref, odd_out, even_out):
+    blocks = (before_ref, own_ref, after_ref)
+    odd_out[...] = packed_gram(members, blocks, wo_ref)
+    even_out[...] = packed_gram(members, blocks, we_ref)
+
+
+def own_kernel(members, tiles, before_ref, own_ref, after_ref, w_ref, x_ref, gram_out, mean_ref, pert_ref, wide):
+    gram_out[...] = packed_gram(members, (before_ref, own_ref, after_ref), w_ref)
     wide[...] = x_ref[...].astype(F32)
     extra = pert_ref.shape[0] - members
     pert_ref[members:, :] = jnp.zeros((extra, pert_ref.shape[1]), BF16)
@@ -274,8 +276,7 @@
     chunks = width // LANES
     cand_rows = 9 * chunks
 
-    own_row = lax.axis_index("mem")
-    side = jnp.stack([own_row % 2, lax.axis_index("reg") % 2]).astype(jnp.int32)
+    side = (lax.axis_index("reg") % 2).astype(jnp.int32).reshape(1)
     weight_shape = jax.ShapeDtypeStruct((3 * chunks, LANES), F32)
     weight, weight_odd, weight_even = call(
         weight_kernel,
@@ -305,7 +306,7 @@
     state = lax.all_to_all(packed, "mem", split_axis=0, concat_axis=0, tiled=True)
     state = state.reshape(members * tiles, LANES)
 
-    index = lax.dynamic_slice_in_dim(obs_index[0], own_row, 1, axis=0)
+    index = lax.dynamic_slice_in_dim(obs_index[0], lax.axis_index("mem"), 1, axis=0)
     wide = [pltpu.VMEM((members * tiles, LANES), F32)]
     observed = call(
         functools.partial(observe_kernel, tiles),
@@ -314,21 +315,20 @@
         flops=2 * members * cells * width,
         nbytes=2 * members * cells,
     )(state, index, yobs[0], weight_odd, weight_even)
-    rows_in = (side, observed, swap(observed, "mem", 1), swap(observed, "mem", 0))
+    size = lax.axis_size("mem")
+    up = [(i, (i + 1) % size) for i in range(size)]
+    before = lax.ppermute(observed, "mem", up)
+    after = lax.ppermute(observed, "mem", [(j, i) for i, j in up])
+    rows_in = (before, observed, after)
     gram_shape = jax.ShapeDtypeStruct((2 * LANES, LANES), F32)
-
-    def to_neighbour(place, weights):
-        partial = call(
-            functools.partial(neighbour_kernel, members),
-            gram_shape,
-            flops=6 * members * padded * width,
-            nbytes=8 * members * padded,
-            in_specs=[SCALARS] + [WHOLE] * 4,
-        )(*rows_in, weights)
-        return swap(partial, "reg", place)
-
-    odd_gram = to_neighbour(1, weight_odd)
-    even_gram = to_neighbour(0, weight_even)
+    odd_part, even_part = call(
+        functools.partial(neighbour_kernel, members),
+        (gram_shape,) * 2,
+        flops=12 * members * padded * width,
+        nbytes=8 * members * padded,
+    )(*rows_in, weight_odd, weight_even)
+    odd_gram = swap(odd_part, "reg", 1)
+    even_gram = swap(even_part, "reg", 0)
     gram, mean, pert = call(
         functools.partial(own_kernel, members, tiles),
         (
@@ -339,7 +339,6 @@
         wide,
         flops=6 * members * padded * width,
         nbytes=8 * members * cells,
-        in_specs=[SCALARS] + [WHOLE] * 5,
     )(*rows_in, weight, state)
     analysis = call(
         functools.partial(update_kernel, members, tiles),

time: 97.9 us -> 96.8 us (0.989)
  waiting for transfers between devices: 13.4 us -> 17.4 us
  starting transfers between devices: 41.5 us -> 37.7 us
  Pallas kernels: 11.7 us -> 9.31 us
  blocking collectives: 29.2 us -> 31.1 us
    ppermute x6 -> x4, starting transfers between devices: 24.8 us -> 18.4 us  [swap(): return lax.ppermute(block, axis, pairs + [(j, i) for i, j in pairs])]
    ppermute x0 -> x2, waiting for transfers between devices: none -> 3.32 us  [the longest x1 3.19 us: local(): after = lax.ppermute(observed, 'mem', [(j, i) for i, j in up])]
    ppermute x0 -> x2, starting transfers between devices: none -> 2.63 us  [the longest x1 2.62 us: local(): after = lax.ppermute(observed, 'mem', [(j, i) for i, j in up])]
    all_to_all x1, blocking collectives: 29.2 us -> 31.1 us  [local(): lax.all_to_all(analysis.reshape(regions, rows, LANES), 'mem', split_axis=...]
    pallas_call x2 -> x1, Pallas kernels: 2.06 us -> 0.73 us  [local(): call(functools.partial(neighbour_kernel, members), (gram_shape,) * 2, flo...]
    all_to_all x1, waiting for transfers between devices: 6.81 us -> 8.01 us  [local(): lax.all_to_all(packed, 'mem', split_axis=0, concat_axis=0, tiled=True)]
    ppermute x6 -> x4, waiting for transfers between devices: 6.54 us -> 6.11 us  [swap(): return lax.ppermute(block, axis, pairs + [(j, i) for i, j in pairs])]
  transfers between devices with their start and end apart: 7 -> 7, of which waited for: 4 -> 5; matrix products, arithmetic and copies ran while one was open for 0% -> 0% of each run, Pallas kernels for 4% -> 1%
where the time goes in v4:
time: 96.8 us; the launch traced here: 96.4 us
  starting transfers between devices  37.7 us (39%)
  blocking collectives  31.1 us (32%)
  waiting for transfers between devices  17.4 us (18%)
  Pallas kernels  9.31 us (10%)
    all_to_all x1, blocking collectives, local(): lax.all_to_all(analysis.reshape(regions, rows, LANES), 'mem', split_axis=...  31.1 us
    ppermute x4, starting transfers between devices, swap(): return lax.ppermute(block, axis, pairs + [(j, i) for i, j in pairs])  18.4 us
    all_to_all x1, starting transfers between devices, local(): lax.all_to_all(packed, 'mem', split_axis=0, concat_axis=0, tiled=True)  16.7 us
    all_to_all x1, waiting for transfers between devices, local(): lax.all_to_all(packed, 'mem', split_axis=0, concat_axis=0, tiled=True)  8.01 us
    ppermute x4, waiting for transfers between devices, swap(): return lax.ppermute(block, axis, pairs + [(j, i) for i, j in pairs])  6.11 us
    pallas_call x1, Pallas kernels, local(): call(functools.partial(update_kernel, members, tiles), jax.ShapeDtypeStru...  3.43 us
    ppermute x1, waiting for transfers between devices, local(): after = lax.ppermute(observed, 'mem', [(j, i) for i, j in up])  3.19 us
    ppermute x1, starting transfers between devices, local(): after = lax.ppermute(observed, 'mem', [(j, i) for i, j in up])  2.62 us
  transfers between devices with their start and end apart: 7, of which 5 were waited for; matrix products, arithmetic and copies ran while one was open for 0% of the time, Pallas kernels for 1%

profile of v4, /device:TPU:1, one launch (start us, length us, event | category | flops | bytes accessed | tf_op | source)
XLA Modules:
  0.0 96.4 jit_solution(105574542757692947)
XLA Ops:
  0.0 0.0 copy-start
  0.0 2.0 %shard_map.64 = bf16[24,80,128]{2,1,0:T(8,128)(2,1)} custom-call(bf16[10,24576]{1,0:T(8,128)(2,1)} %bitcast.16), custom_call_target="tpu_custom_call" | custom-call | bytes 983040 | tf_op jit(solution)/shard_map/pallas_call | solution.py:291
  2.0 16.7 %all-to-all-start = ((bf16[24,80,128]{2,1,0:T(8,128)(2,1)}), bf16[24,80,128]{2,1,0:T(8,128)(2,1)S(1)}, u32[]{:S(2)}, u32[]{:S(2)}) async-start(bf16[24,80,128]{2,1,0:T(8,128)(2,1)} %shard_map.64), calls=%async_computation | async-start | bytes 983040 | tf_op jit(solution)/shard_map/all_to_all | solution.py:306
  18.7 0.0 copy-start.2
  18.7 0.0 copy-start.1
  19.4 0.0 copy-done.2
  19.4 0.0 copy-done.1
  19.4 0.7 shard_map.65
  20.2 7.3 %collective-permute-start = (f32[12,128]{1,0:T(8,128)S(1)}, f32[12,128]{1,0:T(8,128)S(1)}, u32[]{:S(2)}, u32[]{:S(2)}) collective-permute-start(f32[12,128]{1,0:T(8,128)S(1)} %get-tuple-element.13), channel_id=1, source_target_pairs={{1,2},{3,4},{5,6},{7,8},{9,10},{11,12},{13,14},{15,16},{17,18},{19... | collective-permute-start | bytes 18440 | tf_op jit(solution)/shard_map/ppermute | solution.py:40
  27.5 1.9 %collective-permute-start.1 = (f32[12,128]{1,0:T(8,128)S(1)}, f32[12,128]{1,0:T(8,128)S(1)}, u32[]{:S(2)}, u32[]{:S(2)}) collective-permute-start(f32[12,128]{1,0:T(8,128)S(1)} %get-tuple-element.14), channel_id=1, source_target_pairs={{0,1},{2,3},{4,5},{6,7},{8,9},{10,11},{12,13},{14,15},{16,17},{18,... | collective-permute-start | bytes 18440 | tf_op jit(solution)/shard_map/ppermute | solution.py:40
  29.4 0.0 copy-done
  29.4 0.0 copy-start.3
  29.4 0.0 collective-permute-done.wo_ref
  29.4 2.7 %collective-permute-done.1.we_ref = f32[12,128]{1,0:T(8,128)S(1)} collective-permute-done((f32[12,128]{1,0:T(8,128)S(1)}, f32[12,128]{1,0:T(8,128)S(1)}, u32[]{:S(2)}, u32[]{:S(2)}) %collective-permute-start.1) | collective-permute-done | bytes 6176 | tf_op jit(solution)/shard_map/ppermute | solution.py:40
  32.1 8.0 %all-to-all-done = bf16[24,80,128]{2,1,0:T(8,128)(2,1)S(1)} async-done(((bf16[24,80,128]{2,1,0:T(8,128)(2,1)}), bf16[24,80,128]{2,1,0:T(8,128)(2,1)S(1)}, u32[]{:S(2)}, u32[]{:S(2)}) %all-to-all-start) | async-done | bytes 491552 | tf_op jit(solution)/shard_map/all_to_all | solution.py:306
  40.2 0.0 copy-done.3
  40.2 0.8 shard_map.66.own_ref
  40.9 2.6 %collective-permute-start.3 = (bf16[256,512]{1,0:T(8,128)(2,1)S(1)}, bf16[256,512]{1,0:T(8,128)(2,1)S(1)}, u32[]{:S(2)}, u32[]{:S(2)}) collective-permute-start(bf16[256,512]{1,0:T(8,128)(2,1)S(1)} %shard_map.66.own_ref), channel_id=1, source_target_pairs={{32,0},{64,32},{96,64},{128,96},{160,128},{192,160},{224,192},{256... | collective-permute-start | bytes 786440 | tf_op jit(solution)/shard_map/ppermute | solution.py:321
  43.6 0.0 collective-permute-start.2
  43.6 3.2 %collective-permute-done.3.after_ref = bf16[256,512]{1,0:T(8,128)(2,1)S(1)} collective-permute-done((bf16[256,512]{1,0:T(8,128)(2,1)S(1)}, bf16[256,512]{1,0:T(8,128)(2,1)S(1)}, u32[]{:S(2)}, u32[]{:S(2)}) %collective-permute-start.3) | collective-permute-done | bytes 262176 | tf_op jit(solution)/shard_map/ppermute | solution.py:321
  46.7 0.1 collective-permute-done.2.before_ref
  46.9 0.7 shard_map.68
  47.6 7.3 %collective-permute-start.4 = (f32[256,128]{1,0:T(8,128)S(1)}, f32[256,128]{1,0:T(8,128)S(1)}, u32[]{:S(2)}, u32[]{:S(2)}) collective-permute-start(f32[256,128]{1,0:T(8,128)S(1)} %get-tuple-element.17), channel_id=1, source_target_pairs={{1,2},{3,4},{5,6},{7,8},{9,10},{11,12},{13,14},{15,16},{17,18},{19... | collective-permute-start | bytes 393224 | tf_op jit(solution)/shard_map/ppermute | solution.py:40
  54.9 1.9 %collective-permute-start.5 = (f32[256,128]{1,0:T(8,128)S(1)}, f32[256,128]{1,0:T(8,128)S(1)}, u32[]{:S(2)}, u32[]{:S(2)}) collective-permute-start(f32[256,128]{1,0:T(8,128)S(1)} %get-tuple-element.18), channel_id=1, source_target_pairs={{0,1},{2,3},{4,5},{6,7},{8,9},{10,11},{12,13},{14,15},{16,17},{18,... | collective-permute-start | bytes 393224 | tf_op jit(solution)/shard_map/ppermute | solution.py:40
  56.8 0.7 shard_map.67
  57.5 0.0 collective-permute-done.4.odd_ref
  57.5 3.4 %collective-permute-done.5.even_ref = f32[256,128]{1,0:T(8,128)S(1)} collective-permute-done((f32[256,128]{1,0:T(8,128)S(1)}, f32[256,128]{1,0:T(8,128)S(1)}, u32[]{:S(2)}, u32[]{:S(2)}) %collective-permute-start.5) | collective-permute-done | bytes 131104 | tf_op jit(solution)/shard_map/ppermute | solution.py:40
  60.9 3.4 %shard_map.69 = bf16[1920,128]{1,0:T(8,128)(2,1)S(1)} custom-call(f32[256,128]{1,0:T(8,128)S(1)} %get-tuple-element.16.g_ref, f32[256,128]{1,0:T(8,128)S(1)} %collective-permute-done.4.odd_ref, f32[256,128]{1,0:T(8,128)S(1)} %collective-permute-done.5.even_ref, f32[1,1024]{1,0:T(1,128)S(1)} %get-tuple-element.19.mean_ref, ...), custom_call_target="tpu_custom_call" | custom-call | flops 1223884800 | bytes 983040 | tf_op jit(solution)/shard_map/pallas_call | solution.py:343
  64.3 31.1 %all_to_all.10.x_ref = bf16[24,80,128]{2,1,0:T(8,128)(2,1)S(1)} all-to-all(bf16[24,80,128]{2,1,0:T(8,128)(2,1)S(1)} %bitcast.12), channel_id=1, replica_groups=mesh['mem'=24,'reg'=32] {'mem'}, dimensions={0} | all-to-all | bytes 983040 | tf_op jit(solution)/shard_map/all_to_all | solution.py:350
  95.4 1.0 %shard_map.70 = bf16[10,24576]{1,0:T(8,128)(2,1)} custom-call(bf16[24,80,128]{2,1,0:T(8,128)(2,1)S(1)} %all_to_all.10.x_ref), custom_call_target="tpu_custom_call" | custom-call | bytes 983040 | tf_op jit(solution)/shard_map/pallas_call | solution.py:353
  (1 shorter events, 0.0 us)
Async XLA Ops:
  0.0 29.4 %copy-start = (s32[1,24,512]{2,1,0:T(8,128)S(1)}, s32[1,24,512]{2,1,0:T(8,128)}, u32[]{:S(2)}) copy-start(s32[1,24,512]{2,1,0:T(8,128)} %param.7) | copy-start | bytes 147460
  2.0 38.1 %all-to-all-start = ((bf16[24,80,128]{2,1,0:T(8,128)(2,1)}), bf16[24,80,128]{2,1,0:T(8,128)(2,1)S(1)}, u32[]{:S(2)}, u32[]{:S(2)}) async-start(bf16[24,80,128]{2,1,0:T(8,128)(2,1)} %shard_map.64), calls=%async_computation | async-start | bytes 983040 | tf_op jit(solution)/shard_map/all_to_all | solution.py:306
  18.7 0.7 copy-start.2
  18.7 0.7 copy-start.1
  20.2 9.3 %collective-permute-start = (f32[12,128]{1,0:T(8,128)S(1)}, f32[12,128]{1,0:T(8,128)S(1)}, u32[]{:S(2)}, u32[]{:S(2)}) collective-permute-start(f32[12,128]{1,0:T(8,128)S(1)} %get-tuple-element.13), channel_id=1, source_target_pairs={{1,2},{3,4},{5,6},{7,8},{9,10},{11,12},{13,14},{15,16},{17,18},{19... | collective-permute-start | bytes 18440 | tf_op jit(solution)/shard_map/ppermute | solution.py:40
  27.5 4.7 %collective-permute-start.1 = (f32[12,128]{1,0:T(8,128)S(1)}, f32[12,128]{1,0:T(8,128)S(1)}, u32[]{:S(2)}, u32[]{:S(2)}) collective-permute-start(f32[12,128]{1,0:T(8,128)S(1)} %get-tuple-element.14), channel_id=1, source_target_pairs={{0,1},{2,3},{4,5},{6,7},{8,9},{10,11},{12,13},{14,15},{16,17},{18,... | collective-permute-start | bytes 18440 | tf_op jit(solution)/shard_map/ppermute | solution.py:40
  29.4 10.7 %copy-start.3 = (bf16[1,1,512]{2,1,0:T(2,128)(2,1)S(1)}, bf16[1,1,512]{2,1,0:T(2,128)(2,1)}, u32[]{:S(2)}) copy-start(bf16[1,1,512]{2,1,0:T(2,128)(2,1)} %param.8) | copy-start | bytes 3076
  40.9 5.8 %collective-permute-start.3 = (bf16[256,512]{1,0:T(8,128)(2,1)S(1)}, bf16[256,512]{1,0:T(8,128)(2,1)S(1)}, u32[]{:S(2)}, u32[]{:S(2)}) collective-permute-start(bf16[256,512]{1,0:T(8,128)(2,1)S(1)} %shard_map.66.own_ref), channel_id=1, source_target_pairs={{32,0},{64,32},{96,64},{128,96},{160,128},{192,160},{224,192},{256... | collective-permute-start | bytes 786440 | tf_op jit(solution)/shard_map/ppermute | solution.py:321
  43.6 3.3 %collective-permute-start.2 = (bf16[256,512]{1,0:T(8,128)(2,1)S(1)}, bf16[256,512]{1,0:T(8,128)(2,1)S(1)}, u32[]{:S(2)}, u32[]{:S(2)}) collective-permute-start(bf16[256,512]{1,0:T(8,128)(2,1)S(1)} %shard_map.66.own_ref), channel_id=1, source_target_pairs={{0,32},{32,64},{64,96},{96,128},{128,160},{160,192},{192,224},{224... | collective-permute-start | bytes 786440 | tf_op jit(solution)/shard_map/ppermute | solution.py:320
  47.6 9.9 %collective-permute-start.4 = (f32[256,128]{1,0:T(8,128)S(1)}, f32[256,128]{1,0:T(8,128)S(1)}, u32[]{:S(2)}, u32[]{:S(2)}) collective-permute-start(f32[256,128]{1,0:T(8,128)S(1)} %get-tuple-element.17), channel_id=1, source_target_pairs={{1,2},{3,4},{5,6},{7,8},{9,10},{11,12},{13,14},{15,16},{17,18},{19... | collective-permute-start | bytes 393224 | tf_op jit(solution)/shard_map/ppermute | solution.py:40
  54.9 6.0 %collective-permute-start.5 = (f32[256,128]{1,0:T(8,128)S(1)}, f32[256,128]{1,0:T(8,128)S(1)}, u32[]{:S(2)}, u32[]{:S(2)}) collective-permute-start(f32[256,128]{1,0:T(8,128)S(1)} %get-tuple-element.18), channel_id=1, source_target_pairs={{0,1},{2,3},{4,5},{6,7},{8,9},{10,11},{12,13},{14,15},{16,17},{18,... | collective-permute-start | bytes 393224 | tf_op jit(solution)/shard_map/ppermute | solution.py:40
